TPU v7x, 32 devices: a whole 2x2x4 slice. The times are simulated.
32 devices in a mesh: batch: 4 (over z), seq: 8 (over y, x, core).
Axes of the slice: x: 2, y: 2, z: 4, core: 2. Of those that a mesh axis runs over, the one named last changes fastest.
Arguments:
- tokens: bfloat16 [48, 1024, 768], P('batch', 'seq'), may hold values from -6 to 6
- attend_weight: bfloat16 [768, 2304], P('batch'), may hold values from -0.3125 to 0.3125
- query_bias: bfloat16 [768], P('batch'), may hold values from -3 to 3
- value_bias: bfloat16 [768], P('batch'), may hold values from -3 to 3
- output_weight: bfloat16 [768, 768], P('batch'), may hold values from -0.625 to 0.625
- output_bias: bfloat16 [768], P('batch'), may hold values from -3 to 3
- first_gain: bfloat16 [768], P('batch'), may hold values from 0.5 to 1.5
- first_shift: bfloat16 [768], P('batch'), may hold values from -3 to 3
- expand_weight: bfloat16 [768, 3072], P('batch'), may hold values from -0.21875 to 0.21875
- expand_bias: bfloat16 [3072], P('batch'), may hold values from -3 to 3
- reduce_weight: bfloat16 [3072, 768], P('batch'), may hold values from -0.109375 to 0.109375
- reduce_bias: bfloat16 [768], P('batch'), may hold values from -3 to 3
- second_gain: bfloat16 [768], P('batch'), may hold values from 0.5 to 1.5
- second_shift: bfloat16 [768], P('batch'), may hold values from -3 to 3
- query_rank: int32 [48, 12, 1024], P('batch', None, 'seq'), may hold values from 0 to 1023, as said below
- key_rank: int32 [48, 12, 1024], P('batch', None, 'seq'), may hold values from 0 to 1023, as said below
- cotangent: bfloat16 [48, 1024, 768], P('batch', 'seq'), may hold values from -6 to 6
Outputs:
- layer_out: bfloat16 [48, 1024, 768], P('batch', 'seq')
- token_grad: bfloat16 [48, 1024, 768], P('batch', 'seq')
- attend_weight_grad: float32 [768, 2304], P('batch')
- query_bias_grad: float32 [768], P('batch')
- value_bias_grad: float32 [768], P('batch')
- output_weight_grad: float32 [768, 768], P('batch')
- output_bias_grad: float32 [768], P('batch')
- first_gain_grad: float32 [768], P('batch')
- first_shift_grad: float32 [768], P('batch')
- expand_weight_grad: float32 [768, 3072], P('batch')
- expand_bias_grad: float32 [3072], P('batch')
- reduce_weight_grad: float32 [3072, 768], P('batch')
- reduce_bias_grad: float32 [768], P('batch')
- second_gain_grad: float32 [768], P('batch')
- second_shift_grad: float32 [768], P('batch')
Inputs may be any that keep to these rules, and one draw needn't show every extreme that they name: `query_rank`: for each sequence and head a permutation of the token places; place p lies in cluster p // 128. Of the 128 tokens of each aligned block j * 128 to (j + 1) * 128 - 1 of a sequence, exactly 16 lie in each cluster. `key_rank`: drawn independently of query_rank under the same rules.
All inputs are finite; a program needn't handle non-finite values.
Results may differ from a plain program's by a relative error of at most 0.02.
Values may be sent and summed in bfloat16 or wider, within the bound.
A program may use at most 256 MiB of HBM per device.

v0:
```python
import functools
import math

import jax
import jax.numpy as jnp
from jax import lax
from jax.experimental import pallas as pl
from jax.experimental.pallas import tpu as pltpu
from jax.sharding import PartitionSpec as P

epsilon = 1e-05


def layer_norm(resid, gain, shift):
    center = jnp.mean(resid, axis=-1, keepdims=True)
    centered = resid - center
    spread = jnp.mean(centered * centered, axis=-1, keepdims=True)
    inverse = lax.rsqrt(spread + epsilon)
    normed = centered * inverse
    return (normed * gain + shift, normed, inverse)


def norm_back(upstream, normed, inverse, gain):
    scaled = upstream * gain
    first_mean = jnp.mean(scaled, axis=-1, keepdims=True)
    second_mean = jnp.mean(scaled * normed, axis=-1, keepdims=True)
    return inverse * (scaled - first_mean - normed * second_mean)


def gelu_slope(value):
    cumulative = 0.5 * (1.0 + lax.erf(value * 0.5**0.5))
    density = jnp.exp(-0.5 * value * value) * (2.0 * math.pi) ** (-0.5)
    return cumulative + value * density


def transpose_left(first, second):
    return lax.dot_general(
        first, second, (((0,), (0,)), ((), ())), preferred_element_type=jnp.float32
    )


def transpose_right(first, second):
    return lax.dot_general(
        first, second, (((1,), (1,)), ((), ())), preferred_element_type=jnp.float32
    )


def group_table(rank, cluster, owners):
    share = cluster // owners
    target = rank // cluster
    length = rank.shape[-1]
    places = lax.broadcasted_iota(jnp.int32, (length, length), 0)
    later = lax.broadcasted_iota(jnp.int32, (length, length), 1)
    before = (places < later)[None, None]
    same = target[..., :, None] == target[..., None, :]
    earlier = jnp.sum((same & before).astype(jnp.int32), axis=-2)
    position = target * share + earlier
    slots = lax.broadcasted_iota(jnp.int32, position.shape + (length,), 3)
    return (position[..., None] == slots).astype(jnp.bfloat16)


def sort_heads(rows, table, heads):
    seqs, length, width = rows.shape
    split = rows.reshape(seqs, length, heads, width // heads)
    moved = jnp.einsum("shtp,sthd->sphd", table, split, preferred_element_type=jnp.float32)
    return moved.astype(rows.dtype).reshape(seqs, length, width)


def unsort_heads(rows, table, heads):
    seqs, length, width = rows.shape
    split = rows.reshape(seqs, length, heads, width // heads)
    moved = jnp.einsum("shtp,sphd->sthd", table, split, preferred_element_type=jnp.float32)
    return moved.astype(rows.dtype).reshape(seqs, length, width)


def cluster_scores(queries, keys_rows, heads):
    items, length, width = queries.shape
    size = width // heads
    query_split = queries.reshape(items, length, heads, size)
    key_split = keys_rows.reshape(items, length, heads, size)
    scores = jnp.einsum(
        "sqhd,skhd->shqk", query_split, key_split, preferred_element_type=jnp.float32
    )
    return scores * size ** (-0.5)


def cluster_forward(queries, keys_rows, values_rows, heads):
    items, length, width = queries.shape
    scores = cluster_scores(queries, keys_rows, heads)
    top = jnp.max(scores, axis=-1, keepdims=True)
    weights = jnp.exp(scores - top)
    total = jnp.sum(weights, axis=-1, keepdims=True)
    probs = (weights / total).astype(jnp.bfloat16)
    value_split = values_rows.reshape(items, length, heads, width // heads)
    context = jnp.einsum("shqk,skhd->sqhd", probs, value_split, preferred_element_type=jnp.float32)
    return (
        context.reshape(items, length, width).astype(jnp.bfloat16),
        (top + jnp.log(total))[..., 0],
    )


def cluster_backward(scores, log_total, queries, keys_rows, values_rows, grad_context, heads):
    items, length, width = queries.shape
    size = width // heads
    query_split = queries.reshape(items, length, heads, size)
    key_split = keys_rows.reshape(items, length, heads, size)
    value_split = values_rows.reshape(items, length, heads, size)
    grad_split = grad_context.reshape(items, length, heads, size)
    probs = jnp.exp(scores - log_total[..., None])
    grad_probs = jnp.einsum(
        "sqhd,skhd->shqk", grad_split, value_split, preferred_element_type=jnp.float32
    )
    inner = jnp.sum(probs * grad_probs, axis=-1, keepdims=True)
    grad_scores = (probs * (grad_probs - inner)).astype(jnp.bfloat16)
    scale = size ** (-0.5)
    grad_query = (
        jnp.einsum("shqk,skhd->sqhd", grad_scores, key_split, preferred_element_type=jnp.float32)
        * scale
    )
    grad_key = (
        jnp.einsum("shqk,sqhd->skhd", grad_scores, query_split, preferred_element_type=jnp.float32)
        * scale
    )
    grad_value = jnp.einsum(
        "shqk,sqhd->skhd",
        probs.astype(jnp.bfloat16),
        grad_split,
        preferred_element_type=jnp.float32,
    )
    shape = (items, length, width)
    return (
        grad_query.reshape(shape).astype(jnp.bfloat16),
        grad_key.reshape(shape).astype(jnp.bfloat16),
        grad_value.reshape(shape).astype(jnp.bfloat16),
    )


def send_context(context):
    return lax.all_to_all(context, "seq", split_axis=1, concat_axis=1, tiled=True)


def send_grads(grads):
    return (
        lax.all_to_all(grads[0], "seq", split_axis=1, concat_axis=1, tiled=True),
        lax.all_to_all(grads[1], "seq", split_axis=1, concat_axis=1, tiled=True),
        lax.all_to_all(grads[2], "seq", split_axis=1, concat_axis=1, tiled=True),
    )


def make_step(left, pieces):
    total = jnp.dot(left, pieces[0], preferred_element_type=jnp.float32)
    stored = tuple(pieces[1:]) + ()
    placed = tuple((piece for piece in stored))
    return (total,) + placed


def make_hidden_step(before, pieces):
    section = before + pieces[1].astype(jnp.float32)
    activated = jax.nn.gelu(section, approximate=False).astype(jnp.bfloat16)
    total = jnp.dot(activated, pieces[0], preferred_element_type=jnp.float32)
    stored = ()
    return (total, section, activated) + stored


def per_device(
    tokens,
    attend_weight,
    query_bias,
    value_bias,
    output_weight,
    output_bias,
    first_gain,
    first_shift,
    expand_weight,
    expand_bias,
    reduce_weight,
    reduce_bias,
    second_gain,
    second_shift,
    query_rank,
    key_rank,
    cotangent,
):
    seqs, cluster, width = tokens.shape
    heads = query_rank.shape[1]
    rows = seqs * cluster
    owners = lax.axis_size("seq")
    flat = tokens.reshape(rows, width)
    attend_out = make_step(
        flat,
        (
            lax.all_gather(attend_weight, "batch", axis=0, tiled=True),
            lax.all_gather(query_bias, "batch", axis=0, tiled=True),
            lax.all_gather(value_bias, "batch", axis=0, tiled=True),
        ),
    )
    summed = attend_out[0]
    queries = (summed[:, :width] + attend_out[1].astype(jnp.float32)).astype(jnp.bfloat16)
    keys_rows = summed[:, width : 2 * width].astype(jnp.bfloat16)
    values_rows = (summed[:, 2 * width :] + attend_out[2].astype(jnp.float32)).astype(jnp.bfloat16)
    query_table = group_table(query_rank, cluster, owners)
    key_table = group_table(key_rank, cluster, owners)
    query_sorted = sort_heads(queries.reshape(seqs, cluster, width), query_table, heads)
    key_sorted = sort_heads(keys_rows.reshape(seqs, cluster, width), key_table, heads)
    value_sorted = sort_heads(values_rows.reshape(seqs, cluster, width), key_table, heads)
    received = (
        lax.all_to_all(query_sorted, "seq", split_axis=1, concat_axis=1, tiled=True),
        lax.all_to_all(key_sorted, "seq", split_axis=1, concat_axis=1, tiled=True),
        lax.all_to_all(value_sorted, "seq", split_axis=1, concat_axis=1, tiled=True),
    )
    context, log_total = cluster_forward(received[0], received[1], received[2], heads)
    forward_out = (send_context(context), log_total, received[0], received[1], received[2])
    context_rows = unsort_heads(forward_out[0], query_table, heads).reshape(rows, width)
    output_out = make_step(
        context_rows,
        (
            lax.all_gather(output_weight, "batch", axis=0, tiled=True),
            lax.all_gather(output_bias, "batch", axis=0, tiled=True),
            lax.all_gather(first_gain, "batch", axis=0, tiled=True),
            lax.all_gather(first_shift, "batch", axis=0, tiled=True),
        ),
    )
    resid_one = flat.astype(jnp.float32) + output_out[0] + output_out[1].astype(jnp.float32)
    gain_one = output_out[2].astype(jnp.float32)
    middle, normed_one, inverse_one = layer_norm(
        resid_one, gain_one, output_out[3].astype(jnp.float32)
    )
    middle_low = middle.astype(jnp.bfloat16)
    expand_out = make_step(
        middle_low,
        (
            lax.all_gather(expand_weight, "batch", axis=0, tiled=True),
            lax.all_gather(reduce_bias, "batch", axis=0, tiled=True),
            lax.all_gather(second_gain, "batch", axis=0, tiled=True),
            lax.all_gather(second_shift, "batch", axis=0, tiled=True),
        ),
    )
    hidden_out = make_hidden_step(
        expand_out[0],
        (
            lax.all_gather(reduce_weight, "batch", axis=0, tiled=True),
            lax.all_gather(expand_bias, "batch", axis=0, tiled=True),
        ),
    )
    pre_full, hidden_full = (hidden_out[1], hidden_out[2])
    resid_two = middle + hidden_out[0] + expand_out[1].astype(jnp.float32)
    gain_two = expand_out[2].astype(jnp.float32)
    final, normed_two, inverse_two = layer_norm(
        resid_two, gain_two, expand_out[3].astype(jnp.float32)
    )
    layer_out = final.astype(jnp.bfloat16).reshape(seqs, cluster, width)
    attend_full, output_full, expand_full, reduce_full = (
        lax.all_gather(attend_weight, "batch", axis=0, tiled=True),
        lax.all_gather(output_weight, "batch", axis=0, tiled=True),
        lax.all_gather(expand_weight, "batch", axis=0, tiled=True),
        lax.all_gather(reduce_weight, "batch", axis=0, tiled=True),
    )
    upstream = cotangent.reshape(rows, width).astype(jnp.float32)
    grad_second_gain = jnp.sum(upstream * normed_two, axis=0)
    grad_second_shift = jnp.sum(upstream, axis=0)
    grad_resid_two = norm_back(upstream, normed_two, inverse_two, gain_two)
    grad_branch_two = grad_resid_two.astype(jnp.bfloat16)
    grad_reduce_bias = jnp.sum(grad_branch_two, axis=0, dtype=jnp.float32)
    grad_reduce = transpose_left(hidden_full, grad_branch_two)
    grad_hidden = transpose_right(grad_branch_two, reduce_full)
    grad_pre = (grad_hidden * gelu_slope(pre_full)).astype(jnp.bfloat16)
    grad_expand_bias = jnp.sum(grad_pre, axis=0, dtype=jnp.float32)
    grad_expand = transpose_left(middle_low, grad_pre)
    grad_middle = grad_resid_two + transpose_right(grad_pre, expand_full)
    grad_first_gain = jnp.sum(grad_middle * normed_one, axis=0)
    grad_first_shift = jnp.sum(grad_middle, axis=0)
    grad_resid_one = norm_back(grad_middle, normed_one, inverse_one, gain_one)
    grad_branch_one = grad_resid_one.astype(jnp.bfloat16)
    grad_output_bias = jnp.sum(grad_branch_one, axis=0, dtype=jnp.float32)
    grad_output = transpose_left(context_rows, grad_branch_one)
    grad_context = transpose_right(grad_branch_one, output_full).astype(jnp.bfloat16)
    grad_sorted = sort_heads(grad_context.reshape(seqs, cluster, width), query_table, heads)
    grad_received = lax.all_to_all(grad_sorted, "seq", split_axis=1, concat_axis=1, tiled=True)
    kept_scores = cluster_scores(forward_out[2], forward_out[3], heads)
    home = send_grads(
        cluster_backward(
            kept_scores,
            forward_out[1],
            forward_out[2],
            forward_out[3],
            forward_out[4],
            grad_received,
            heads,
        )
    )
    grad_queries = unsort_heads(home[0], query_table, heads).reshape(rows, width)
    grad_keys = unsort_heads(home[1], key_table, heads).reshape(rows, width)
    grad_values = unsort_heads(home[2], key_table, heads).reshape(rows, width)
    grad_mixed = jnp.concatenate([grad_queries, grad_keys, grad_values], axis=1)
    grad_query_bias = jnp.sum(grad_queries, axis=0, dtype=jnp.float32)
    grad_value_bias = jnp.sum(grad_values, axis=0, dtype=jnp.float32)
    grad_attend = transpose_left(flat, grad_mixed)
    token_grad = (
        (grad_resid_one + transpose_right(grad_mixed, attend_full))
        .astype(jnp.bfloat16)
        .reshape(seqs, cluster, width)
    )
    owned = (
        lax.psum_scatter(
            grad_attend.astype(jnp.bfloat16), "batch", scatter_dimension=0, tiled=True
        ).astype(jnp.float32),
        lax.psum_scatter(
            grad_query_bias.astype(jnp.bfloat16), "batch", scatter_dimension=0, tiled=True
        ).astype(jnp.float32),
        lax.psum_scatter(
            grad_value_bias.astype(jnp.bfloat16), "batch", scatter_dimension=0, tiled=True
        ).astype(jnp.float32),
        lax.psum_scatter(
            grad_output.astype(jnp.bfloat16), "batch", scatter_dimension=0, tiled=True
        ).astype(jnp.float32),
        lax.psum_scatter(
            grad_output_bias.astype(jnp.bfloat16), "batch", scatter_dimension=0, tiled=True
        ).astype(jnp.float32),
        lax.psum_scatter(
            grad_first_gain.astype(jnp.bfloat16), "batch", scatter_dimension=0, tiled=True
        ).astype(jnp.float32),
        lax.psum_scatter(
            grad_first_shift.astype(jnp.bfloat16), "batch", scatter_dimension=0, tiled=True
        ).astype(jnp.float32),
        lax.psum_scatter(
            grad_expand.astype(jnp.bfloat16), "batch", scatter_dimension=0, tiled=True
        ).astype(jnp.float32),
        lax.psum_scatter(
            grad_expand_bias.astype(jnp.bfloat16), "batch", scatter_dimension=0, tiled=True
        ).astype(jnp.float32),
        lax.psum_scatter(
            grad_reduce.astype(jnp.bfloat16), "batch", scatter_dimension=0, tiled=True
        ).astype(jnp.float32),
        lax.psum_scatter(
            grad_reduce_bias.astype(jnp.bfloat16), "batch", scatter_dimension=0, tiled=True
        ).astype(jnp.float32),
        lax.psum_scatter(
            grad_second_gain.astype(jnp.bfloat16), "batch", scatter_dimension=0, tiled=True
        ).astype(jnp.float32),
        lax.psum_scatter(
            grad_second_shift.astype(jnp.bfloat16), "batch", scatter_dimension=0, tiled=True
        ).astype(jnp.float32),
    )
    shared = (
        lax.psum(owned[0].astype(jnp.bfloat16), "seq").astype(jnp.float32),
        lax.psum(owned[1].astype(jnp.bfloat16), "seq").astype(jnp.float32),
        lax.psum(owned[2].astype(jnp.bfloat16), "seq").astype(jnp.float32),
        lax.psum(owned[3].astype(jnp.bfloat16), "seq").astype(jnp.float32),
        lax.psum(owned[4].astype(jnp.bfloat16), "seq").astype(jnp.float32),
        lax.psum(owned[5].astype(jnp.bfloat16), "seq").astype(jnp.float32),
        lax.psum(owned[6].astype(jnp.bfloat16), "seq").astype(jnp.float32),
        lax.psum(owned[7].astype(jnp.bfloat16), "seq").astype(jnp.float32),
        lax.psum(owned[8].astype(jnp.bfloat16), "seq").astype(jnp.float32),
        lax.psum(owned[9].astype(jnp.bfloat16), "seq").astype(jnp.float32),
        lax.psum(owned[10].astype(jnp.bfloat16), "seq").astype(jnp.float32),
        lax.psum(owned[11].astype(jnp.bfloat16), "seq").astype(jnp.float32),
        lax.psum(owned[12].astype(jnp.bfloat16), "seq").astype(jnp.float32),
    )
    return (
        layer_out,
        token_grad,
        shared[0],
        shared[1],
        shared[2],
        shared[3],
        shared[4],
        shared[5],
        shared[6],
        shared[7],
        shared[8],
        shared[9],
        shared[10],
        shared[11],
        shared[12],
    )


MESH = pl.DeviceIdType.MESH
f32 = jnp.float32
bf16 = jnp.bfloat16


class Place:
    def __init__(self, chips, depth):
        self.chips, self.depth = chips, depth
        self.z = lax.axis_index("batch")
        spot = lax.axis_index("seq")
        self.chip, self.core = lax.div(spot, 2), lax.rem(spot, 2)

    def chip_at(self, k):
        return lax.rem(self.chip + k + self.chips, self.chips)

    def z_at(self, k):
        return lax.rem(self.z + k + self.depth, self.depth)

    def plane(self, k):
        return (self.z, self.chip_at(k) * 2 + self.core)

    def tower(self, k):
        return (self.z_at(k), self.chip * 2 + self.core)

    def sibling(self):
        return (self.z, self.chip * 2 + 1 - self.core)

    def greet(self):
        bell = pltpu.get_barrier_semaphore()
        others = [self.plane(k) for k in range(1, self.chips)]
        others += [self.tower(k) for k in range(1, self.depth)]
        others.append(self.sibling())
        for other in others:
            pl.semaphore_signal(bell, inc=1, device_id=other, device_id_type=MESH)
        pl.semaphore_wait(bell, len(others))


def far_copy(src, dst, sems, at, device):
    return pltpu.make_async_remote_copy(
        src_ref=src,
        dst_ref=dst,
        send_sem=sems[0].at[at],
        recv_sem=sems[1].at[at],
        device_id=device,
        device_id_type=MESH,
    )


def one_hot(row, slots):
    return jnp.where(slots == row, 1.0, 0.0).astype(bf16)


def split_lanes(tile, low):
    zero = jnp.zeros_like(tile)
    return jnp.where(low, tile, zero), jnp.where(low, zero, tile)


def stack_lanes(tile, low):
    first, second = split_lanes(tile, low)
    return jnp.concatenate([first, second], axis=0)


def dot_rows(a, b):
    return jnp.dot(a, b, preferred_element_type=f32)


def dot_lanes(a, b):
    return lax.dot_general(a, b, (((1,), (1,)), ((), ())), preferred_element_type=f32)


def dot_first(a, b):
    return lax.dot_general(a, b, (((0,), (0,)), ((), ())), preferred_element_type=f32)


def multiple(value, by):
    return pl.multiple_of(value, by)


def forward_kernel(
    chips,
    depth,
    heads,
    tok_ref,
    pos_ref,
    aw_ref,
    vec_ref,
    ow_ref,
    ew_ref,
    rw_ref,
    cot_ref,
    x_out,
    ctx_out,
    q_out,
    k_out,
    v_out,
    p_out,
    pos_out,
    aw_out,
    vec_out,
    ow_out,
    ew_out,
    rw_out,
    n1_out,
    inv_out,
    ml_out,
    hid_out,
    slope_out,
    lo_out,
    gr_out,
    gb_out,
    sum_out,
    xbuf,
    posbuf,
    wbuf,
    vbuf,
    bias,
    ctxb,
    ctxt,
    owbuf,
    ewbuf,
    rwbuf,
    cbuf,
    n1buf,
    invbuf,
    mlbuf,
    vecs,
    upb,
    sums,
    tok_s,
    tok_r,
    tokc_s,
    tokc_r,
    pos_s,
    pos_r,
    posc_s,
    posc_r,
    up_s,
    up_r,
    dn_s,
    dn_r,
    awc_s,
    awc_r,
    vec_s,
    vec_r,
    wz_s,
    wz_r,
    wp_s,
    wp_r,
    wd_s,
    wd_r,
    wc_s,
    wc_r,
    ctx_s,
    ctx_r,
    cot_s,
    cot_r,
    oc_s,
    oc_r,
    loc,
    out_sem,
    slope_sem,
    att_sem,
):
    me = Place(chips, depth)
    z, chip, core = me.z, me.chip, me.core
    per = tok_ref.shape[0] // chips
    half = aw_ref.shape[1] // 6
    rows_z = aw_ref.shape[0]
    pairs = heads // 4
    size = half // (2 * pairs)
    me.greet()

    def aw_block(zz):
        return wbuf.at[pl.ds(multiple(zz * rows_z, 8), rows_z)]

    def up_copy(h):
        return far_copy(
            aw_block(z - h), aw_block(z - h), (up_s, up_r), h, (z + 1, chip * 2 + core)
        )

    def down_copy(h):
        return far_copy(
            aw_block(z + h), aw_block(z + h), (dn_s, dn_r), h, (z - 1, chip * 2 + core)
        )

    def up_got(h):
        return far_copy(
            aw_block(z - 1 - h), aw_block(z - 1 - h), (up_s, up_r), h, me.sibling()
        )

    def down_got(h):
        return far_copy(
            aw_block(z + 1 + h), aw_block(z + 1 + h), (dn_s, dn_r), h, me.sibling()
        )

    def pass_on():
        @pl.when(z < depth - 1)
        def _():
            up_copy(0).start()

        @pl.when(z > 0)
        def _():
            down_copy(0).start()

    def pass_rest():
        for h in range(depth - 1):

            @pl.when(z > h)
            def _():
                up_got(h).wait_recv()
                if h + 1 < depth - 1:

                    @pl.when(z < depth - 1)
                    def _():
                        up_copy(h + 1).start()

            @pl.when(z + 1 + h < depth)
            def _():
                down_got(h).wait_recv()
                if h + 1 < depth - 1:

                    @pl.when(z > 0)
                    def _():
                        down_copy(h + 1).start()

    def pass_end():
        for h in range(depth - 1):

            @pl.when((z >= h) & (z < depth - 1))
            def _():
                up_copy(h).wait_send()

            @pl.when((z + h < depth) & (z > 0))
            def _():
                down_copy(h).wait_send()

    def mine(ref, target):
        return ref.at[pl.ds(target * per, per)]

    def tok_copy(k):
        return far_copy(
            mine(tok_ref, me.chip_at(k)), xbuf.at[core, chip], (tok_s, tok_r), k - 1, me.plane(k)
        )

    def pos_copy(k):
        return far_copy(
            mine(pos_ref, me.chip_at(k)), posbuf.at[core, chip], (pos_s, pos_r), k - 1, me.plane(k)
        )

    def vec_copy(k):
        return far_copy(vec_ref, vbuf.at[z], (vec_s, vec_r), k - 1, me.tower(k))

    sends = []
    for k in range(1, chips):
        sends.append(pos_copy(k))
        sends[-1].start()
    for k in range(1, depth):
        sends.append(vec_copy(k))
        sends[-1].start()
    for k in range(1, chips):
        sends.append(tok_copy(k))
        sends[-1].start()
    local = []

    def keep(src, dst):
        copy = pltpu.make_async_copy(src, dst, loc.at[len(local)])
        copy.start()
        local.append(copy)

    for part in range(3):
        keep(
            aw_ref.at[:, pl.ds(multiple(part * 2 * half + core * half, 128), half)],
            wbuf.at[pl.ds(multiple(z * rows_z, 8), rows_z), pl.ds(part * half, half)],
        )
    keep(mine(tok_ref, chip), xbuf.at[core, chip])
    keep(mine(pos_ref, chip), posbuf.at[core, chip])
    keep(vec_ref, vbuf.at[z])
    for copy in local[:3]:
        copy.wait()
    pass_on()
    wide = ew_ref.shape[1] // (2 * chips)
    tall = rw_ref.shape[0] // (2 * chips)
    mid_rows = rows_z // 2
    mine_at = core * chips + chip

    def piece(kind):
        if kind == 0:
            return ow_ref.at[pl.ds(multiple(core * mid_rows, 8), mid_rows)]
        if kind == 1:
            return ew_ref.at[:, pl.ds(multiple(mine_at * wide, 128), wide)]
        return rw_ref.at[pl.ds(multiple(mine_at * tall, 8), tall)]

    def place(kind, zz):
        if kind == 0:
            return owbuf.at[zz, core]
        if kind == 1:
            return ewbuf.at[zz, :, pl.ds(multiple(mine_at * wide, 128), wide)]
        return rwbuf.at[zz, mine_at]

    def place_all(kind, at):
        if kind == 1:
            return ewbuf.at[:, :, pl.ds(multiple(at * wide, 128), wide)]
        return rwbuf.at[:, at]

    for kind in range(3):
        keep(piece(kind), place(kind, z))

    def wz_copy(kind, k):
        return far_copy(
            piece(kind),
            place(kind, z),
            (wz_s, wz_r),
            kind * (depth - 1) + k - 1,
            me.tower(k),
        )

    beside = (chip + 1 - 2 * lax.rem(chip, 2), lax.rem(chip + 2, chips))
    across = chips - 1 - chip

    def part_of(kind, origin, side):
        at = core * chips + origin
        span = pl.ds(side * (depth // 2), depth // 2)
        if kind == 1:
            return ewbuf.at[span, :, pl.ds(multiple(at * wide, 128), wide)]
        return rwbuf.at[span, at]

    def wp_copy(kind, d):
        spot = place_all(kind, mine_at)
        return far_copy(
            spot, spot, (wp_s, wp_r), (kind - 1) * 2 + d, (z, beside[d] * 2 + core)
        )

    def wd_copy(kind, d):
        spot = part_of(kind, beside[d], d)
        return far_copy(
            spot, spot, (wd_s, wd_r), (kind - 1) * 2 + d, (z, beside[1 - d] * 2 + core)
        )

    def wc_copy(kind, n):
        at = core * chips + (chip, beside[0], beside[1], across)[n]
        return far_copy(
            place_all(kind, at),
            place_all(kind, at),
            (wc_s, wc_r),
            (kind - 1) * chips + n,
            me.sibling(),
        )

    def oc_copy():
        spot = owbuf.at[:, core]
        return far_copy(spot, spot, (oc_s, oc_r), 0, me.sibling())

    def cot_copy(k):
        return far_copy(
            mine(cot_ref, me.chip_at(k)), cbuf.at[chip], (cot_s, cot_r), k - 1, me.plane(k)
        )

    keep(mine(cot_ref, chip), cbuf.at[chip])

    for copy in local[3:5]:
        copy.wait()

    def tokc_copy(k):
        source = me.chip_at(-k)
        return far_copy(
            xbuf.at[core, source], xbuf.at[core, source], (tokc_s, tokc_r), k, me.sibling()
        )

    def posc_copy(k):
        source = me.chip_at(-k)
        return far_copy(
            posbuf.at[core, source], posbuf.at[core, source], (posc_s, posc_r), k, me.sibling()
        )

    for k in range(chips):
        if k:
            pos_copy(k).wait_recv()
            tok_copy(k).wait_recv()
        for copy in (posc_copy(k), tokc_copy(k)):
            copy.start()
            sends.append(copy)
    for k in range(1, chips):
        cot_copy(k).start()
        sends.append(cot_copy(k))
    pass_rest()
    for k in range(1, depth):
        wz_copy(1, k).start()
        for kind in range(3):
            sends.append(wz_copy(kind, k))
    for k in range(1, depth):
        vec_copy(k).wait_recv()
    for k in range(chips):
        posc_copy(k).wait_recv()
        tokc_copy(k).wait_recv()
    for copy in local[5:]:
        copy.wait()

    outs = []

    def emit(src, dst):
        copy = pltpu.make_async_copy(src, dst, out_sem.at[len(outs)])
        copy.start()
        outs.append(copy)

    emit(xbuf, x_out)
    emit(posbuf, pos_out)
    emit(wbuf, aw_out.at[core])
    awc = far_copy(wbuf, aw_out.at[core], (awc_s, awc_r), 0, me.sibling())
    awc.start()
    sends.append(awc)

    quarter = rows_z
    for zz in range(depth):
        begin = zz * quarter
        for row, at in ((0, 0), (1, 2)):
            for side in range(2):
                lo = max(begin, side * half)
                hi = min(begin + quarter, (side + 1) * half)
                if lo < hi:
                    bias[side, 0:1, at * half + lo - side * half : at * half + hi - side * half] = (
                        vbuf[zz, row : row + 1, lo - begin : hi - begin]
                    )
    bias[0, 0:1, half : 2 * half] = jnp.zeros((1, half), f32)
    bias[1, 0:1, half : 2 * half] = jnp.zeros((1, half), f32)
    added = bias[core, 0:1, :]
    for zz in range(depth):
        for row in range(8):
            vecs[row : row + 1, zz * quarter : (zz + 1) * quarter] = vbuf[
                zz, row : row + 1, :quarter
            ]
        steps = upb.shape[1] // (depth * quarter)
        for row in range(steps):
            to = (zz * steps + row) * quarter
            upb[0:1, to : to + quarter] = vbuf[zz, 8 + row : 9 + row, :quarter]

    cluster = tok_ref.shape[1]
    blocks = 2 * chips
    share = cluster // blocks
    width = tok_ref.shape[2]

    slots = lax.broadcasted_iota(jnp.int32, (cluster, cluster), 0)
    low = lax.broadcasted_iota(jnp.int32, (cluster, 128), 1) < size
    scale = size ** (-0.5)

    def tables(jj, i, pair, part):
        first = part * heads + core * (heads // 2) + 2 * pair
        rows = [
            one_hot(posbuf[jj // chips, jj % chips, i, pl.ds(first + h, 1), :], slots)
            for h in range(2)
        ]
        return rows

    def tower_wait(kind):
        for k in range(1, depth):
            wz_copy(kind, k).wait_recv()

    def plane_first(kind):
        for d in range(2):
            wp_copy(kind, d).start()
        wc_copy(kind, 0).start()

    def plane_second(kind):
        for d in range(2):
            wp_copy(kind, d).wait_recv()
            wd_copy(kind, d).start()
            wc_copy(kind, 1 + d).start()

    def plane_last(kind):
        for d in range(2):
            wd_copy(kind, d).wait_recv()
        wc_copy(kind, 3).start()
        for n in range(chips):
            wc_copy(kind, n).wait()
        for d in range(2):
            wp_copy(kind, d).wait_send()
            wd_copy(kind, d).wait_send()

    def hook(i, pair):
        step = i * pairs + pair
        last = per * pairs - 1

        @pl.when(step == min(1, last))
        def _():
            tower_wait(1)
            plane_first(1)
            for k in range(1, depth):
                wz_copy(2, k).start()

        @pl.when(step == min(5, last))
        def _():
            tower_wait(2)
            for k in range(1, depth):
                wz_copy(0, k).start()

        @pl.when(step == min(7, last))
        def _():
            plane_second(1)
            plane_first(2)

    def attention(qkv, qs, ks, vs, ps, os):
        @pl.loop(0, blocks)
        def _(jj):
            x = xbuf[lax.div(jj, chips), lax.rem(jj, chips)].reshape(per * cluster, width)
            mixed = (dot_rows(x, wbuf[...]) + added).astype(bf16)
            for at in range(3 * pairs):
                qkv[at, jj] = mixed[:, at * 128 : (at + 1) * 128].reshape(per, cluster, 128)

        @pl.loop(0, per)
        def _(i):
            @pl.loop(0, pairs)
            def _(pair):
                at = i * pairs + pair
                for jj in range(blocks):
                    tq = jnp.concatenate(tables(jj, i, pair, 0), axis=1)
                    tk = jnp.concatenate(tables(jj, i, pair, 1), axis=1)
                    q = stack_lanes(qkv[pair, jj, i], low)
                    k = stack_lanes(qkv[pairs + pair, jj, i], low)
                    v = stack_lanes(qkv[2 * pairs + pair, jj, i], low)
                    span = slice(jj * share, (jj + 1) * share)
                    sq = dot_rows(tq, q).astype(bf16)
                    skv = dot_rows(tk, jnp.concatenate([k, v], axis=1)).astype(bf16)
                    qs[at, :, span, :] = sq.reshape(blocks, share, 128)
                    ks[at, :, span, :] = skv[:, :128].reshape(blocks, share, 128)
                    vs[at, :, span, :] = skv[:, 128:].reshape(blocks, share, 128)
                for c in range(blocks):
                    scores = dot_lanes(qs[at, c], stack_lanes(ks[at, c], low)) * scale
                    halves = []
                    for h in range(2):
                        s = scores[:, h * cluster : (h + 1) * cluster]
                        e = jnp.exp(s - jnp.max(s, axis=1, keepdims=True))
                        halves.append((e / jnp.sum(e, axis=1, keepdims=True)).astype(bf16))
                    probs = jnp.concatenate(halves, axis=1)
                    ps[at, c] = probs
                    o = dot_rows(probs, stack_lanes(vs[at, c], low)).astype(bf16)
                    os[c] = o
                for jj in range(blocks):
                    tq = jnp.concatenate(tables(jj, i, pair, 0), axis=0)
                    rows = os[:, jj * share : (jj + 1) * share, :].reshape(cluster, 128)
                    back = dot_first(tq, stack_lanes(rows, low)).astype(bf16)
                    ctxb[jj // chips, jj % chips, i, :, pl.ds(multiple(pair * 128, 128), 128)] = back
                hook(i, pair)

        pieces = ((qs, q_out), (ks, k_out), (vs, v_out), (ps, p_out))
        copies = [
            pltpu.make_async_copy(src, dst, att_sem.at[n]) for n, (src, dst) in enumerate(pieces)
        ]
        far, own = ctx_copies()
        for copy in copies + [far, own]:
            copy.start()
        for copy in copies + [far, own]:
            copy.wait()

    def ctx_copies():
        lanes = pl.ds(multiple(core * half, 128), half)
        far = far_copy(
            ctxb.at[1 - core], ctxt.at[:, :, :, lanes], (ctx_s, ctx_r), 0, me.sibling()
        )
        own = pltpu.make_async_copy(ctxb.at[core], ctxt.at[:, :, :, lanes], att_sem.at[4])
        return far, own

    group = (per * pairs, blocks, cluster, 128)
    pl.run_scoped(
        attention,
        pltpu.VMEM((3 * pairs, blocks, per, cluster, 128), bf16),
        pltpu.VMEM(group, bf16),
        pltpu.VMEM(group, bf16),
        pltpu.VMEM(group, bf16),
        pltpu.VMEM((per * pairs, blocks, cluster, 2 * cluster), bf16),
        pltpu.VMEM((blocks, cluster, 128), bf16),
    )

    tower_wait(0)
    oc_copy().start()
    oc_copy().wait()
    emit(ctxt, ctx_out)
    context_out = outs[-1]
    emit(owbuf, ow_out)
    tile = per * cluster
    hidden = upb.shape[1]
    eps = epsilon

    def moments(rows):
        center = jnp.mean(rows, axis=1, keepdims=True)
        centered = rows - center
        spread = jnp.mean(centered * centered, axis=1, keepdims=True)
        inverse = lax.rsqrt(spread + eps)
        return centered * inverse, inverse

    def slope_out_copy(j, slot):
        return pltpu.make_async_copy(sbuf.at[slot], slope_out.at[j], slope_sem.at[slot])

    def vec(row):
        return vecs[row : row + 1, :]

    def feed(hbuf, sbuf):
        step = sbuf.shape[3]

        def slope_copy(n):
            return pltpu.make_async_copy(
                sbuf.at[n % 2],
                slope_out.at[:, :, pl.ds(n * step, step)],
                slope_sem.at[n % 2],
            )

        @pl.loop(0, chips)
        def _(j):
            rows = ctxt[j].reshape(tile, width)
            branch = dot_rows(rows, owbuf[...].reshape(width, width))
            resid = xbuf[core, j].reshape(tile, width).astype(f32) + branch + vec(2)
            normed, inverse = moments(resid)
            n1buf[j] = normed
            invbuf[j] = jnp.broadcast_to(inverse, (tile, 128))
            mlbuf[j] = (normed * vec(3) + vec(4)).astype(bf16).reshape(per, cluster, width)

        plane_last(1)
        emit(ewbuf, ew_out)
        for n in range(hidden // step):
            lanes = slice(n * step, (n + 1) * step)
            if n >= 2:
                slope_copy(n - 2).wait()
            for j in range(chips):
                weight = ewbuf[:, :, lanes].reshape(width, step)
                pre = dot_rows(mlbuf[j].reshape(tile, width), weight) + upb[0:1, lanes]
                cumulative = 0.5 * (1.0 + lax.erf(pre * 0.5**0.5))
                density = jnp.exp(-0.5 * pre * pre) * (2.0 * math.pi) ** (-0.5)
                hbuf[j, :, lanes] = (pre * cumulative).astype(bf16)
                sbuf[n % 2, j] = (cumulative + pre * density).astype(bf16)
            slope_copy(n).start()
            if n == 1:
                plane_second(2)

        emit(vecs, vec_out)
        held = len(outs)
        emit(n1buf, n1_out)
        emit(invbuf, inv_out)
        emit(mlbuf, ml_out)
        emit(hbuf, hid_out)
        plane_last(2)
        pass_end()
        emit(rwbuf, rw_out)
        for k in range(1, chips):
            cot_copy(k).wait_recv()
        sums[...] = jnp.zeros_like(sums)
        waited = (context_out, outs[held])
        for copy in waited:
            copy.wait()

        @pl.loop(0, chips)
        def _(j):
            branch = vec(5)
            for zz in range(depth):
                span = hidden // depth
                branch = branch + dot_rows(
                    hbuf[j, :, zz * span : (zz + 1) * span], rwbuf[zz].reshape(span, width)
                )
            middle = n1buf[j] * vec(3) + vec(4)
            normed, inverse = moments(middle + branch)
            upstream = cbuf[j].reshape(tile, width).astype(f32)
            cbuf[j] = (normed * vec(6) + vec(7)).astype(bf16).reshape(per, cluster, width)
            sums[0:1, :] += jnp.sum(upstream * normed, axis=0, keepdims=True)
            sums[1:2, :] += jnp.sum(upstream, axis=0, keepdims=True)
            scaled = upstream * vec(6)
            first = jnp.mean(scaled, axis=1, keepdims=True)
            second = jnp.mean(scaled * normed, axis=1, keepdims=True)
            grad = inverse * (scaled - first - normed * second)
            n1buf[j] = grad
            low_grad = grad.astype(bf16)
            sums[2:3, :] += jnp.sum(low_grad.astype(f32), axis=0, keepdims=True)
            ctxt[j] = low_grad.reshape(per, cluster, width)

        emit(cbuf, lo_out)
        emit(n1buf, gr_out)
        emit(ctxt, gb_out)
        emit(sums, sum_out)
        for copy in sends:
            copy.wait_send()
        awc.wait_recv()
        for n in range(max(hidden // step - 2, 0), hidden // step):
            slope_copy(n).wait()
        for copy in outs:
            if not any(copy is other for other in waited):
                copy.wait()

    pl.run_scoped(
        feed,
        pltpu.VMEM((chips, tile, hidden), bf16),
        pltpu.VMEM((2, chips, tile, hidden // depth), bf16),
    )


def forward(
    tokens,
    pos,
    attend_weight,
    vectors,
    output_weight,
    expand_weight,
    reduce_weight,
    cotangent,
    chips,
    depth,
    heads,
):
    seqs, cluster, width = tokens.shape
    per, blocks, pairs = seqs // chips, 2 * chips, heads // 4
    half = width // 2
    rows_z = attend_weight.shape[0]
    hidden = expand_weight.shape[1]
    items = per * pairs
    tile = per * cluster
    dma = pltpu.SemaphoreType.DMA
    anywhere = pl.BlockSpec(memory_space=pl.ANY)
    tall = reduce_weight.shape[0] // blocks
    shapes = [
        ((2, chips, per, cluster, width), bf16),
        ((chips, per, cluster, width), bf16),
        ((items, blocks, cluster, 128), bf16),
        ((items, blocks, cluster, 128), bf16),
        ((items, blocks, cluster, 128), bf16),
        ((items, blocks, cluster, 2 * cluster), bf16),
        ((2, chips, per, 2 * heads, cluster), jnp.int32),
        ((2, depth * rows_z, 3 * half), bf16),
        ((8, width), f32),
        ((depth, 2, rows_z // 2, width), bf16),
        ((depth, rows_z, hidden), bf16),
        ((depth, blocks, tall, width), bf16),
        ((chips, tile, width), f32),
        ((chips, tile, 128), f32),
        ((chips, per, cluster, width), bf16),
        ((chips, tile, hidden), bf16),
        ((chips, tile, hidden), bf16),
        ((chips, per, cluster, width), bf16),
        ((chips, tile, width), f32),
        ((chips, per, cluster, width), bf16),
        ((8, width), f32),
    ]
    t, c = depth - 1, chips - 1
    vm = pltpu.VMEM
    return pl.pallas_call(
        functools.partial(forward_kernel, chips, depth, heads),
        out_shape=[jax.ShapeDtypeStruct(*s) for s in shapes],
        in_specs=[anywhere] * 8,
        out_specs=[anywhere] * len(shapes),
        scratch_shapes=[
            vm(shapes[0][0], bf16),
            vm(shapes[6][0], jnp.int32),
            vm(shapes[7][0][1:], bf16),
            vm((depth,) + vectors.shape, f32),
            vm((2, 8, 3 * half), f32),
            vm((2, chips, per, cluster, half), bf16),
            vm(shapes[1][0], bf16),
            vm(shapes[9][0], bf16),
            vm(shapes[10][0], bf16),
            vm(shapes[11][0], bf16),
            vm(shapes[17][0], bf16),
            vm(shapes[12][0], f32),
            vm(shapes[13][0], f32),
            vm(shapes[14][0], bf16),
            vm((8, width), f32),
            vm((8, hidden), f32),
            vm((8, width), f32),
            dma((c,)), dma((c,)), dma((chips,)), dma((chips,)),
            dma((c,)), dma((c,)), dma((chips,)), dma((chips,)),
            dma((t,)), dma((t,)), dma((t,)), dma((t,)), dma((1,)), dma((1,)),
            dma((t,)), dma((t,)),
            dma((3 * t,)), dma((3 * t,)),
            dma((4,)), dma((4,)), dma((4,)), dma((4,)),
            dma((2 * chips,)), dma((2 * chips,)),
            dma((1,)), dma((1,)),
            dma((c,)), dma((c,)),
            dma((1,)), dma((1,)),
            dma((12,)), dma((24,)), dma((2,)), dma((5,)),
        ],
        compiler_params=pltpu.CompilerParams(
            collective_id=1, has_side_effects=True, vmem_limit_bytes=63 * 2**20
        ),
        name="forward",
    )(
        tokens,
        pos,
        attend_weight,
        vectors,
        output_weight,
        expand_weight,
        reduce_weight,
        cotangent,
    )


def add_into(target, at, parts):
    total = target[at].astype(f32)
    for part in parts:
        total = total + part.astype(f32)
    target[at] = total.astype(target.dtype)


class Reducer:
    def __init__(self, me, own, other, near, mid, last, done, sems, tower_first):
        self.me, self.own, self.other = me, own, other
        self.near, self.mid, self.last, self.done = near, mid, last, done
        (self.near_s, self.near_r, self.mid_s, self.mid_r, self.last_s, self.last_r) = sems[:6]
        (self.back_s, self.back_r, self.side_s, self.side_r) = sems[6:10]
        self.tower_first = tower_first
        self.sizes = (mid.shape[0] + 1, last.shape[0] + 1)

    def spot(self, axis, k):
        me = self.me
        if self.tower_first == (axis == 0):
            return me.z_at(k), me.tower(k)
        return me.chip_at(k), me.plane(k)

    def near_copy(self, a):
        return far_copy(
            self.other.at[a], self.near.at[a], (self.near_s, self.near_r), a, self.me.sibling()
        )

    def fold_near(self, a):
        self.near_copy(a).wait_recv()
        for b in range(self.sizes[1]):
            add_into(self.own, (a, b), [self.near[a, b]])

    def mid_copy(self, k):
        where, device = self.spot(0, k)
        return far_copy(
            self.own.at[where], self.mid.at[k - 1], (self.mid_s, self.mid_r), k - 1, device
        )

    def send_mid(self):
        for k in range(1, self.sizes[0]):
            self.mid_copy(k).start()

    def fold_mid(self):
        for k in range(1, self.sizes[0]):
            self.mid_copy(k).wait()
        here = self.spot(0, 0)[0]
        for b in range(self.sizes[1]):
            add_into(self.own, (here, b), [self.mid[k - 1, b] for k in range(1, self.sizes[0])])

    def last_copy(self, k):
        here = self.spot(0, 0)[0]
        where, device = self.spot(1, k)
        return far_copy(
            self.own.at[here, where],
            self.last.at[k - 1],
            (self.last_s, self.last_r),
            k - 1,
            device,
        )

    def send_last(self):
        for k in range(1, self.sizes[1]):
            self.last_copy(k).start()

    def fold_last(self):
        me = self.me
        for k in range(1, self.sizes[1]):
            self.last_copy(k).wait()
        total = self.own[self.spot(0, 0)[0], self.spot(1, 0)[0]].astype(f32)
        for k in range(1, self.sizes[1]):
            total = total + self.last[k - 1].astype(f32)
        self.done[me.core, me.chip] = total.astype(bf16)

    def back_copy(self, k):
        me = self.me
        spot = self.done.at[me.core, me.chip]
        return far_copy(spot, spot, (self.back_s, self.back_r), k - 1, me.plane(k))

    def send_back(self):
        for k in range(1, self.done.shape[1]):
            self.back_copy(k).start()

    def side_copy(self):
        spot = self.done.at[self.me.core]
        return far_copy(spot, spot, (self.side_s, self.side_r), 0, self.me.sibling())

    def send_side(self):
        for k in range(1, self.done.shape[1]):
            self.back_copy(k).wait()
        self.side_copy().start()

    def finish(self):
        self.side_copy().wait()


class Sum:
    def __init__(self, me, vec, got, s, r):
        self.me, self.vec, self.got, self.s, self.r = me, vec, got, s, r

    def copies(self, hop):
        me = self.me
        if hop == 0:
            spots = [(0, me.sibling())]
        elif hop == 1:
            spots = [(k, me.plane(k)) for k in range(1, me.chips)]
        else:
            spots = [(me.chips + k - 1, me.tower(k)) for k in range(1, me.depth)]
        return [far_copy(self.vec, self.got.at[n], (self.s, self.r), n, d) for n, d in spots], spots

    def send(self, hop):
        for copy in self.copies(hop)[0]:
            copy.start()

    def fold(self, hop):
        copies, spots = self.copies(hop)
        for copy in copies:
            copy.wait()
        total = self.vec[...]
        for n, _ in spots:
            total = total + self.got[n]
        self.vec[...] = total


def back_kernel(
    chips,
    depth,
    heads,
    q_ref,
    k_ref,
    v_ref,
    p_ref,
    pos_ref,
    x_ref,
    aw_ref,
    ow_ref,
    ew_ref,
    rw_ref,
    vec_ref,
    ctx_ref,
    n1_ref,
    inv_ref,
    ml_ref,
    hid_ref,
    slope_ref,
    lo_ref,
    gr_ref,
    gb_ref,
    late_ref,
    token_out,
    layer_out,
    aw_out,
    ow_out,
    ew_out,
    rw_out,
    vec_out,
    bias_out,
    dbuf,
    posbuf,
    acc,
    gfar,
    a_mid,
    a_last,
    a_done,
    c_mid,
    c_last,
    c_done,
    o_all,
    o_near,
    o_mid,
    o_last,
    o_done,
    e_all,
    e_near,
    e_mid,
    e_last,
    e_done,
    r_all,
    r_near,
    r_mid,
    r_last,
    r_done,
    vbuf,
    vgot,
    bbuf,
    bgot,
    vecs,
    d_s,
    d_r,
    g_s,
    g_r,
    t_s,
    t_r,
    lo_s,
    lo_r,
    load,
    out_sem,
    v_s,
    v_r,
    b_s,
    b_r,
    *sems,
):
    me = Place(chips, depth)
    z, core, chip = me.z, me.core, me.chip
    per, cluster, width = lo_ref.shape[1:]
    half = width // 2
    pairs = heads // 4
    size = half // (2 * pairs)
    blocks = 2 * chips
    share = cluster // blocks
    tile = per * cluster
    hidden = hid_ref.shape[2]
    wide = hidden // blocks
    strip = width // chips
    quarter = width // depth
    eighth = quarter // blocks
    rows = chips * tile
    me.greet()
    groups = [sems[n * 10 : (n + 1) * 10] for n in range(5)]
    red = Reducer(
        me, r_all.at[core], r_all.at[1 - core], r_near, r_mid, r_last, r_done, groups[0], True
    )
    exp = Reducer(
        me, e_all.at[core], e_all.at[1 - core], e_near, e_mid, e_last, e_done, groups[1], False
    )
    out = Reducer(
        me, o_all.at[core], o_all.at[1 - core], o_near, o_mid, o_last, o_done, groups[2], False
    )
    sums = Sum(me, vbuf, vgot, v_s, v_r)
    biases = Sum(me, bbuf, bgot, b_s, b_r)

    def fetch(src, dst, at):
        return pltpu.make_async_copy(src, dst, load.at[at])

    def lo_copy(k):
        return far_copy(
            lo_ref.at[me.chip_at(k)],
            layer_out.at[pl.ds(chip * per, per)],
            (lo_s, lo_r),
            k - 1,
            me.plane(k),
        )

    lo_keep = pltpu.make_async_copy(
        lo_ref.at[chip], layer_out.at[pl.ds(chip * per, per)], out_sem.at[0]
    )

    block = 2 * wide
    counts = blocks // 2

    def order(n):
        return lax.rem(n + z + chip, counts)

    def fold(n):
        at = order(n)
        red.fold_near(at)
        k = lax.rem(at - z + depth, depth)

        @pl.when(k != 0)
        def _():
            red.mid_copy(k).start()

        @pl.when(lax.div(at, 2) == core)
        def _():
            for side in range(2):
                b = lax.rem(at, 2) * 2 + side
                exp.fold_near(b)
                k = lax.rem(b - chip + chips, chips)

                @pl.when(k != 0)
                def _():
                    exp.mid_copy(k).start()

    def chunks(gb, gbt, mlt, hid, slope, rwc, ewc, gpb):
        def chunk(n, slot):
            at = order(n)
            lanes = pl.ds(multiple(at * block, 128), block)
            return [
                fetch(hid_ref.at[:, :, lanes], hid.at[slot], slot * 4),
                fetch(slope_ref.at[:, :, lanes], slope.at[slot], slot * 4 + 1),
                fetch(rw_ref.at[at], rwc.at[slot], slot * 4 + 2),
                fetch(ew_ref.at[:, :, lanes], ewc.at[slot], slot * 4 + 3),
            ]

        begin = [
            fetch(gb_ref, gb, 8),
            fetch(ml_ref, gpb, 9),
            fetch(gr_ref, acc, 10),
        ]
        later = [
            fetch(vec_ref, vecs, 11),
            fetch(late_ref, vbuf.at[pl.ds(0, 8)], 12),
            fetch(pos_ref, posbuf, 18),
        ]
        for copy in begin + chunk(0, 0) + later:
            copy.start()
        for k in range(1, chips):
            lo_copy(k).start()
        lo_keep.start()
        vbuf[8:, :] = jnp.zeros((blocks, width), f32)
        for copy in begin:
            copy.wait()
        for j in range(chips):
            span = slice(j * tile, (j + 1) * tile)
            mlt[:, span] = jnp.transpose(gpb[j].reshape(tile, width))
            gbt[:, span] = jnp.transpose(gb[j].reshape(tile, width))
        for copy in later:
            copy.wait()

        @pl.loop(0, counts)
        def _(n):
            slot = lax.rem(n, 2)
            at = order(n)
            for copy in chunk(n, slot):
                copy.wait()

            @pl.when(n + 1 < counts)
            def _():
                for copy in chunk(n + 1, 1 - slot):
                    copy.start()

            up = rwc[slot].reshape(block, width)
            down = ewc[slot].reshape(width, block)
            total = jnp.zeros((1, block), f32)
            for j in range(chips):
                grad = dot_lanes(gb[j].reshape(tile, width), up)
                low = (grad * slope[slot, j].astype(f32)).astype(bf16)
                gpb[j] = low.reshape(per, cluster, block)
                acc[j] += dot_lanes(low, down)
                total = total + jnp.sum(low.astype(f32), axis=0, keepdims=True)
            vbuf[pl.ds(8 + at, 1), :block] = total
            term = dot_rows(gbt[...], hid[slot].reshape(rows, block)).astype(bf16)
            for side in range(2):
                r_all[side, at] = term[:, side * wide : (side + 1) * wide].reshape(
                    chips, strip, wide
                )
            red.near_copy(at).start()
            term = dot_rows(mlt[...], gpb[...].reshape(rows, block)).astype(bf16)
            for side in range(2):
                e_all[lax.div(at, 2), lax.rem(at, 2) * 2 + side] = term[
                    :, side * wide : (side + 1) * wide
                ].reshape(depth, quarter, wide)

            @pl.when(lax.div(at, 2) != core)
            def _():
                for side in range(2):
                    exp.near_copy(lax.rem(at, 2) * 2 + side).start()

            @pl.when(n > 0)
            def _():
                fold(n - 1)

    def first_norm(gb, n1, inv, ctx, ow, dsnd):
        later = [
            fetch(ctx_ref, ctx, 13),
            fetch(ow_ref, ow, 14),
            fetch(inv_ref, inv, 15),
        ]
        def n1_copy(j):
            return fetch(n1_ref.at[j], n1.at[j % 2], 16 + j % 2)

        def d_copy(j):
            return far_copy(dsnd.at[j], dbuf.at[core, j], (d_s, d_r), j, me.sibling())

        n1_copy(0).start()
        for copy in later:
            copy.start()
        fold(counts - 1)
        for copy in later:
            copy.wait()
        gain = vecs[3:4, :]
        for row in range(3, 8):
            vbuf[row : row + 1, :] = jnp.zeros((1, width), f32)
        for j in range(chips):
            n1_copy(j).wait()
            if j + 1 < chips:
                n1_copy(j + 1).start()
            grad = acc[j]
            normed = n1[j % 2]
            vbuf[3:4, :] += jnp.sum(grad * normed, axis=0, keepdims=True)
            vbuf[4:5, :] += jnp.sum(grad, axis=0, keepdims=True)
            scaled = grad * gain
            first = jnp.mean(scaled, axis=1, keepdims=True)
            second = jnp.mean(scaled * normed, axis=1, keepdims=True)
            grad = inv[j][:, :1] * (scaled - first - normed * second)
            acc[j] = grad
            low = grad.astype(bf16)
            gb[j] = low.reshape(per, cluster, width)
            vbuf[5:6, :] += jnp.sum(low.astype(f32), axis=0, keepdims=True)
            back = dot_lanes(low, ow[...].reshape(width, width)).astype(bf16)

            for c in range(2):
                piece = back[:, c * half : (c + 1) * half]

                @pl.when(core == c)
                def _():
                    dbuf[c, j] = piece.reshape(per, cluster, half)

                @pl.when(core != c)
                def _():
                    dsnd[j] = piece.reshape(per, cluster, half)

            d_copy(j).start()
        sums.send(0)
        term = dot_first(ctx[...].reshape(rows, width), gb[...].reshape(rows, width))
        for zz in range(depth):
            for c in range(2):
                for p in range(chips):
                    begin_at = zz * quarter + (c * chips + p) * eighth
                    o_all[c, p, zz] = term[begin_at : begin_at + eighth, :].astype(bf16)
        for p in range(chips):
            out.near_copy(p).start()
        for j in range(chips):
            d_copy(j).wait()
        for a in range(depth):
            red.near_copy(a).wait_send()
        for b in range(chips):
            exp.near_copy(b).wait_send()

    shape = (chips, per, cluster, width)
    vm = pltpu.VMEM

    def feed_back(gb):
        pl.run_scoped(
            functools.partial(chunks, gb),
            vm((width, rows), bf16),
            vm((width, rows), bf16),
            vm((2, chips, tile, block), bf16),
            vm((2, chips, tile, block), bf16),
            vm((2, blocks, block // blocks, width), bf16),
            vm((2, depth, quarter, block), bf16),
            vm(shape[:3] + (block,), bf16),
        )
        pl.run_scoped(
            functools.partial(first_norm, gb),
            vm((2, tile, width), f32),
            vm((chips, tile, 128), f32),
            vm(shape, bf16),
            vm((depth, 2, quarter // 2, width), bf16),
            vm((chips, per, cluster, half), bf16),
        )

    pl.run_scoped(feed_back, vm(shape, bf16))

    def attend_back(qs, ks, vs, ps, xbuf, wbuf, ds, gs, gbuf, tbuf, dw, dwa, dwc):
        att = Reducer(me, dwa, None, None, a_mid, a_last, a_done, groups[3], False)
        rest = Reducer(me, dwc, None, None, c_mid, c_last, c_done, groups[4], True)
        cut = dwa.shape[3]

        def loads(i, slot):
            span = pl.ds(i * pairs, pairs)
            pieces = (
                (q_ref.at[span], qs),
                (k_ref.at[span], ks),
                (v_ref.at[span], vs),
                (p_ref.at[span], ps),
            )
            return [fetch(src, dst.at[slot], slot * 4 + n) for n, (src, dst) in enumerate(pieces)]

        def load_x(i):
            return fetch(x_ref.at[:, :, i], xbuf, 8)

        load_w = fetch(aw_ref, wbuf, 9)
        for copy in loads(0, 0) + [load_x(0), load_w]:
            copy.start()
        bbuf[...] = jnp.zeros_like(bbuf)
        slots = lax.broadcasted_iota(jnp.int32, (cluster, cluster), 0)
        low = lax.broadcasted_iota(jnp.int32, (cluster, 128), 1) < size
        scale = size ** (-0.5)

        def tables(jj, i, pair, part):
            begin = part * heads + core * (heads // 2) + 2 * pair
            return [
                one_hot(posbuf[jj // chips, jj % chips, i, pl.ds(begin + h, 1), :], slots)
                for h in range(2)
            ]

        def clusters(i, slot, pair):
            lanes = pl.ds(multiple(pair * 128, 128), 128)
            for jj in range(blocks):
                tq = jnp.concatenate(tables(jj, i, pair, 0), axis=1)
                rows = stack_lanes(dbuf[jj // chips, jj % chips, i, :, lanes], low)
                ds[:, jj * share : (jj + 1) * share, :] = (
                    dot_rows(tq, rows).astype(bf16).reshape(blocks, share, 128)
                )
            for c in range(blocks):
                d = ds[c]
                probs = ps[slot, pair, c]
                slope = dot_lanes(d, stack_lanes(vs[slot, pair, c], low))
                broad = probs.astype(f32)
                halves = []
                for h in range(2):
                    span = slice(h * cluster, (h + 1) * cluster)
                    inner = jnp.sum(broad[:, span] * slope[:, span], axis=1, keepdims=True)
                    halves.append((broad[:, span] * (slope[:, span] - inner)).astype(bf16))
                grads = jnp.concatenate(halves, axis=1)
                gq = dot_rows(grads, stack_lanes(ks[slot, pair, c], low)) * scale
                gk = dot_first(grads, qs[slot, pair, c]) * scale
                gv = dot_first(probs, d)
                gs[0, c] = gq.astype(bf16)
                gs[1, c] = jnp.where(low, gk[:cluster], gk[cluster:]).astype(bf16)
                gs[2, c] = jnp.where(low, gv[:cluster], gv[cluster:]).astype(bf16)
            for jj in range(blocks):
                for part in range(3):
                    if part < 2:
                        table = jnp.concatenate(tables(jj, i, pair, part), axis=0)
                    rows = gs[part, :, jj * share : (jj + 1) * share, :].reshape(cluster, 128)
                    back = dot_first(table, stack_lanes(rows, low))
                    to = pl.ds(multiple(part * half + pair * 128, 128), 128)
                    gbuf[slot, jj // chips, jj % chips, :, to] = back.astype(bf16)

        def give(slot):
            return far_copy(gbuf.at[slot, 1 - core], gfar.at[slot], (g_s, g_r), slot, me.sibling())

        def token_copy(i, slot, k):
            return far_copy(
                tbuf.at[slot, me.chip_at(k)],
                token_out.at[chip * per + i],
                (t_s, t_r),
                i * (chips - 1) + k - 1,
                me.plane(k),
            )

        def token_keep(i, slot):
            return pltpu.make_async_copy(
                tbuf.at[slot, chip], token_out.at[chip * per + i], out_sem.at[1 + i]
            )

        def token_rows(i, slot):
            give(slot).wait()
            for j in range(chips):
                near = dot_lanes(gbuf[slot, core, j], wbuf[core])
                distant = dot_lanes(gfar[slot, j], wbuf[1 - core])
                resid = acc[j, i * cluster : (i + 1) * cluster, :]
                tbuf[slot, j] = (resid + near + distant).astype(bf16)
            token_keep(i, slot).start()
            for k in range(1, chips):
                token_copy(i, slot, k).start()

        ready = []

        def emit(src, dst):
            copy = pltpu.make_async_copy(src, dst, out_sem.at[1 + per + len(ready)])
            copy.start()
            ready.append(copy)

        def step_out_near():
            for p in range(chips):
                out.fold_near(p)
            out.send_mid()
            for p in range(chips):
                out.near_copy(p).wait_send()
            sums.fold(0)
            sums.send(1)

        def step_exp_mid():
            exp.fold_mid()
            exp.send_last()

        def step_red_mid():
            red.fold_mid()
            red.send_last()
            sums.fold(1)
            sums.send(2)

        def step_exp_last():
            exp.fold_last()
            exp.send_back()
            out.fold_mid()
            out.send_last()

        def step_red_last():
            red.fold_last()
            red.send_back()
            sums.fold(2)

        def step_out_last():
            out.fold_last()
            out.send_back()
            exp.send_side()

        def step_sides():
            red.send_side()
            out.send_side()

        hooks = {}
        steps = [
            step_out_near,
            step_exp_mid,
            step_red_mid,
            step_exp_last,
            step_red_last,
            step_out_last,
            step_sides,
        ]
        for n, step in enumerate(steps):
            hooks.setdefault(min(n, per * pairs - 1), []).append(step)

        for i in range(per):
            slot = i % 2
            for copy in loads(i, slot):
                copy.wait()
            if i == 0:
                load_w.wait()
            if i >= 1:
                token_rows(i - 1, 1 - slot)
            if i + 1 < per:
                for copy in loads(i + 1, 1 - slot):
                    copy.start()

            @pl.loop(0, pairs)
            def _(pair):
                clusters(i, slot, pair)
                for n in range(pairs):
                    if hooks.get(i * pairs + n):

                        @pl.when(pair == n)
                        def _():
                            for step in hooks[i * pairs + n]:
                                step()

            if i >= 2:
                token_keep(i - 2, slot).wait()
                for k in range(1, chips):
                    token_copy(i - 2, slot, k).wait()
            give(slot).start()
            load_x(i).wait()
            for b in range(2):
                x = jnp.concatenate([xbuf[b, j] for j in range(chips)], axis=0)
                g = jnp.concatenate([gbuf[slot, b, j] for j in range(chips)], axis=0)
                term = dot_first(x, g)
                if i == 0 and b == 0:
                    dw[...] = term
                else:
                    dw[...] += term
                bbuf[0:1, :] += jnp.sum(g.astype(f32), axis=0, keepdims=True)
            if i + 1 < per:
                load_x(i + 1).start()

        depth_rows = quarter // chips
        for a in range(depth):
            for b in range(chips):
                begin = (a * chips + b) * depth_rows
                dwa[b, a] = dw[begin : begin + depth_rows, :cut].astype(bf16)
                dwc[a, b] = dw[begin : begin + depth_rows, cut:].astype(bf16)
        att.send_mid()
        rest.send_mid()
        biases.send(1)
        token_rows(per - 1, (per - 1) % 2)
        emit(vbuf, vec_out)
        exp.finish()
        for c in range(2):
            for p in range(chips):
                emit(e_done.at[c, p], ew_out.at[:, pl.ds((c * chips + p) * wide, wide)])
        red.finish()
        for c in range(2):
            emit(r_done.at[c], rw_out.at[:, :, pl.ds(c * wide, wide)])
        out.finish()
        emit(o_done, ow_out)
        biases.fold(1)
        biases.send(2)
        att.fold_mid()
        att.send_last()
        rest.fold_mid()
        rest.send_last()
        biases.fold(2)
        share_bias = far_copy(bbuf, bias_out.at[core], (b_s, b_r), 0, me.sibling())
        share_bias.start()
        emit(bbuf, bias_out.at[core])
        att.fold_last()
        att.send_back()
        rest.fold_last()
        rest.send_back()
        att.send_side()
        rest.send_side()
        for reducer, done, begin in ((att, a_done, 0), (rest, c_done, cut)):
            reducer.finish()
            end = begin + done.shape[3]
            for part in range(3):
                lo, hi = max(begin, part * half), min(end, (part + 1) * half)
                for c in range(2):
                    if lo < hi:
                        emit(
                            done.at[c, :, :, pl.ds(lo - begin, hi - lo)],
                            aw_out.at[:, :, pl.ds((part + c) * half + lo, hi - lo)],
                        )
        for i in range(max(per - 2, 0), per):
            token_keep(i, i % 2).wait()
            for k in range(1, chips):
                token_copy(i, i % 2, k).wait()
        share_bias.wait()
        for copy in ready:
            copy.wait()
        lo_keep.wait()
        for k in range(1, chips):
            lo_copy(k).wait()

    group = (2, pairs, blocks, cluster)
    pl.run_scoped(
        attend_back,
        vm(group + (128,), bf16),
        vm(group + (128,), bf16),
        vm(group + (128,), bf16),
        vm(group + (2 * cluster,), bf16),
        vm((2, chips, cluster, width), bf16),
        vm(aw_ref.shape, bf16),
        vm((blocks, cluster, 128), bf16),
        vm((3, blocks, cluster, 128), bf16),
        vm((2, 2, chips, cluster, 3 * half), bf16),
        vm((2, chips, cluster, width), bf16),
        vm((width, 3 * half), f32),
        vm((chips, depth, quarter // chips, a_mid.shape[3]), bf16),
        vm((depth, chips, quarter // chips, c_mid.shape[3]), bf16),
    )


def back(arrays, depth, heads):
    chips, per, cluster, width = arrays[17].shape
    half, blocks = width // 2, 2 * chips
    dma = pltpu.SemaphoreType.DMA
    anywhere = pl.BlockSpec(memory_space=pl.ANY)
    quarter = width // depth
    hidden = arrays[15].shape[2]
    eighth, strip, wide = quarter // blocks, width // chips, hidden // blocks
    rows = quarter // chips
    c, t = chips - 1, depth - 1
    cut = 3 * half // 128 * 5 // 9 * 128
    shapes = [
        ((chips * per, cluster, width), bf16),
        ((chips * per, cluster, width), bf16),
        ((chips, rows, 3 * width), bf16),
        ((2, chips, eighth, width), bf16),
        ((quarter, hidden), bf16),
        ((chips, strip, 2 * wide), bf16),
        ((8 + blocks, width), f32),
        ((2, 8, 3 * half), f32),
    ]
    vm = pltpu.VMEM

    def reducing(near, first, second):
        return [
            dma((near,)), dma((near,)),
            dma((first,)), dma((first,)),
            dma((second,)), dma((second,)),
            dma((c,)), dma((c,)),
            dma((1,)), dma((1,)),
        ]

    return pl.pallas_call(
        functools.partial(back_kernel, chips, depth, heads),
        out_shape=[jax.ShapeDtypeStruct(*s) for s in shapes],
        in_specs=[anywhere] * len(arrays),
        out_specs=[anywhere] * len(shapes),
        scratch_shapes=[
            vm((2, chips, per, cluster, half), bf16),
            vm(arrays[4].shape, jnp.int32),
            vm((chips, per * cluster, width), f32),
            vm((2, chips, cluster, 3 * half), bf16),
            vm((c, depth, rows, cut), bf16),
            vm((t, rows, cut), bf16),
            vm((2, chips, rows, cut), bf16),
            vm((t, chips, rows, 3 * half - cut), bf16),
            vm((c, rows, 3 * half - cut), bf16),
            vm((2, chips, rows, 3 * half - cut), bf16),
            vm((2, chips, depth, eighth, width), bf16),
            vm((chips, depth, eighth, width), bf16),
            vm((c, depth, eighth, width), bf16),
            vm((t, eighth, width), bf16),
            vm((2, chips, eighth, width), bf16),
            vm((2, chips, depth, quarter, wide), bf16),
            vm((chips, depth, quarter, wide), bf16),
            vm((c, depth, quarter, wide), bf16),
            vm((t, quarter, wide), bf16),
            vm((2, chips, quarter, wide), bf16),
            vm((2, depth, chips, strip, wide), bf16),
            vm((depth, chips, strip, wide), bf16),
            vm((t, chips, strip, wide), bf16),
            vm((c, strip, wide), bf16),
            vm((2, chips, strip, wide), bf16),
            vm((8 + blocks, width), f32),
            vm((chips + t, 8 + blocks, width), f32),
            vm((8, 3 * half), f32),
            vm((chips + t, 8, 3 * half), f32),
            vm((8, width), f32),
            dma((chips,)), dma((chips,)), dma((2,)), dma((2,)),
            dma((per * c,)), dma((per * c,)),
            dma((c,)), dma((c,)),
            dma((19,)), dma((1 + per + 16 + blocks,)),
            dma((chips + t,)), dma((chips + t,)), dma((chips + t,)), dma((chips + t,)),
            *reducing(depth, t, c),
            *reducing(chips, c, t),
            *reducing(chips, c, t),
            *reducing(1, c, t),
            *reducing(1, t, c),
        ],
        compiler_params=pltpu.CompilerParams(
            collective_id=2, has_side_effects=True, vmem_limit_bytes=63 * 2**20
        ),
        name="back",
    )(*arrays)


def places(rank, cluster, share):
    seqs, rows, length = rank.shape
    clusters = cluster // share
    target = rank // cluster
    which = lax.broadcasted_iota(jnp.int32, (1, 1, clusters, 1), 2)
    inside = (target[:, :, None, :] == which).astype(bf16)
    first = lax.broadcasted_iota(jnp.int32, (length, length), 0)
    second = lax.broadcasted_iota(jnp.int32, (length, length), 1)
    before = (first < second).astype(bf16)
    count = lax.dot_general(
        inside.reshape(seqs * rows * clusters, length),
        before,
        (((1,), (0,)), ((), ())),
        preferred_element_type=f32,
    ).reshape(seqs, rows, clusters, length)
    spot = which.astype(f32) * share + count
    return jnp.sum(inside.astype(f32) * spot, axis=2).astype(jnp.int32)


def per_chip(
    tokens,
    attend_weight,
    query_bias,
    value_bias,
    output_weight,
    output_bias,
    first_gain,
    first_shift,
    expand_weight,
    expand_bias,
    reduce_weight,
    reduce_bias,
    second_gain,
    second_shift,
    query_rank,
    key_rank,
    cotangent,
):
    seqs, cluster, width = tokens.shape
    heads = query_rank.shape[1]
    owners = lax.axis_size("seq")
    depth = lax.axis_size("batch")
    chips = owners // 2
    half = width // 2
    share = cluster // owners
    pos = places(jnp.concatenate([query_rank, key_rank], axis=1), cluster, share)
    quarter = width // depth
    lines = [
        query_bias,
        value_bias,
        output_bias,
        first_gain,
        first_shift,
        reduce_bias,
        second_gain,
        second_shift,
    ]
    lines += [
        expand_bias[at : at + quarter] for at in range(0, expand_bias.shape[0], quarter)
    ]
    vectors = jnp.zeros((16 * 256,), f32)
    for row, v in enumerate(lines):
        vectors += jnp.pad(v.astype(f32), (row * 256, (16 - row) * 256 - quarter))
    vectors = vectors.reshape(16, 256)
    (
        x_all,
        context,
        qs,
        ks,
        vs,
        ps,
        pos_all,
        attend_all,
        vecs,
        out_all,
        exp_all,
        red_all,
        normed_one,
        inverse_one,
        middle_low,
        hidden,
        slope,
        layer_out,
        grad_resid_two,
        grad_branch_two,
        late_sums,
    ) = forward(
        tokens,
        pos,
        attend_weight,
        vectors,
        output_weight,
        expand_weight,
        reduce_weight,
        cotangent,
        chips,
        depth,
        heads,
    )
    token_grad, layer_out, aw_grad, ow_grad, ew_grad, rw_grad, vec_sum, bias_sum = back(
        (
            qs,
            ks,
            vs,
            ps,
            pos_all,
            x_all,
            attend_all,
            out_all,
            exp_all,
            red_all,
            vecs,
            context,
            normed_one,
            inverse_one,
            middle_low,
            hidden,
            slope,
            layer_out,
            grad_resid_two,
            grad_branch_two,
            late_sums,
        ),
        depth,
        heads,
    )
    z = lax.axis_index("batch")
    six = lax.dynamic_slice_in_dim(vec_sum[:6], z * quarter, quarter, 1)
    up = lax.dynamic_index_in_dim(vec_sum[8:], z, 0, keepdims=False)
    both = jnp.concatenate([bias_sum[0, 0], bias_sum[1, 0]]).reshape(2, 3, half)
    query_value = jnp.transpose(both, (1, 0, 2)).reshape(3, width)
    query_value = lax.dynamic_slice_in_dim(query_value, z * quarter, quarter, 1)
    return (
        layer_out,
        token_grad,
        aw_grad.reshape(quarter, 3 * width).astype(f32),
        query_value[0],
        query_value[2],
        ow_grad.reshape(quarter, width).astype(f32),
        six[5],
        six[3],
        six[4],
        ew_grad.astype(f32),
        up,
        jnp.transpose(rw_grad.reshape(width, -1)).astype(f32),
        six[2],
        six[0],
        six[1],
    )


def layer(mesh):
    def run(*arrays):
        seqs, cluster, width = arrays[0].shape
        heads = arrays[14].shape[1]
        owners, depth = mesh.shape["seq"], mesh.shape["batch"]
        chips = owners // 2
        fits = (
            owners % 2 == 0
            and chips > 1
            and depth == chips == 4
            and seqs % chips == 0
            and cluster == 128
            and heads % 4 == 0
            and width == heads * 64
            and cluster == 16 * owners
            and arrays[8].shape[1] == 4 * width
        )
        return (per_chip if fits else per_device)(*arrays)

    return run


def solution(mesh):
    in_specs = (
        P("batch", "seq", None),
        P("batch", None),
        P("batch"),
        P("batch"),
        P("batch", None),
        P("batch"),
        P("batch"),
        P("batch"),
        P("batch", None),
        P("batch"),
        P("batch", None),
        P("batch"),
        P("batch"),
        P("batch"),
        P("batch", None, "seq"),
        P("batch", None, "seq"),
        P("batch", "seq", None),
    )
    out_specs = (
        P("batch", "seq", None),
        P("batch", "seq", None),
        P("batch", None),
        P("batch"),
        P("batch"),
        P("batch", None),
        P("batch"),
        P("batch"),
        P("batch"),
        P("batch", None),
        P("batch"),
        P("batch", None),
        P("batch"),
        P("batch"),
        P("batch"),
    )
    return jax.shard_map(
        layer(mesh), mesh=mesh, in_specs=in_specs, out_specs=out_specs, check_vma=False
    )
```

profile of v0, /device:TPU:0, one launch (start us, length us, event | category | flops | bytes accessed | tf_op | source)
XLA Modules:
  0.0 330.1 jit_solution(3913250734121975045)
XLA Ops:
  0.6 0.9 fusion.10
  1.6 0.8 convert_add_fusion
  2.3 0.6 reshape.132.vec_ref
  3.0 1.0 add_select_fusion
  4.0 0.6 fusion.1
  4.6 0.7 convert_element_type.81.pos_ref
  5.3 133.4 %forward.1 = (bf16[2,4,3,128,768]{4,3,2,1,0:T(8,128)(2,1)}, bf16[4,3,128,768]{3,2,1,0:T(8,128)(2,1)}, bf16[9,8,128,128]{3,2,1,0:T(8,128)(2,1)}, bf16[9,8,128,128...) custom-call(bf16[12,128,768]{2,1,0:T(8,128)(2,1)} %tok_ref.1, ...), custom_call_target="tpu_custom_call" | custom-call | tf_op jit(solution)/shard_map/forward/pallas_call | solution.py:1116
  138.7 177.0 %back.1 = (bf16[12,128,768]{2,1,0:T(8,128)(2,1)}, bf16[12,128,768]{2,1,0:T(8,128)(2,1)}, bf16[4,48,2304]{2,1,0:T(8,128)(2,1)}, bf16[2,4,24,768]{3,2,1,0:T(8,128)...) custom-call(bf16[9,8,128,128]{3,2,1,0:T(8,128)(2,1)} %get-tuple-elem, ...), custom_call_target="tpu_custom_call" | custom-call | tf_op jit(solution)/shard_map/back/pallas_call | solution.py:1915
  315.7 0.8 slice_reduce_fusion.1
  316.6 0.7 slice.56
  317.3 0.7 fusion.8
  318.0 1.4 bitcast_convert_fusion
  319.4 0.0 copy-start.2
  319.4 2.0 copy.33
  321.4 0.0 copy-start.3
  321.4 0.0 copy-done.2
  321.4 0.0 copy-start.4
  321.4 1.7 convert_element_type.86
  323.1 0.0 copy-start.5
  323.1 0.0 copy-start.1
  323.1 0.0 copy-done.3
  323.1 1.4 bitcast_convert_fusion.1
  324.4 0.0 copy-done.4
  324.5 0.9 bitcast_convert_fusion.2
  325.3 0.0 copy-done.5
  325.3 0.6 dynamic-slice_reduce_fusion
  325.9 0.0 copy-done.1
  325.9 0.0 copy-start
  325.9 1.4 copy.37
  327.4 1.1 copy-done
  328.5 1.4 copy.38
  (5 shorter events, 0.0 us)
Async XLA Ops:
  319.4 2.0 copy-start.2
  321.4 1.7 copy-start.3
  321.4 3.1 copy-start.4
  323.1 2.3 copy-start.5
  323.1 2.9 copy-start.1
  325.9 2.5 copy-start
where the time goes:
time: 334 us; the launch traced here: 330 us
  Pallas kernels  310 us (93%)
  local copies, waits for them, and re-layouts  10.3 us (3%)
  other arithmetic  7.86 us (2%)
    pallas_call x1, Pallas kernels, back(): pl.pallas_call(functools.partial(back_kernel, chips, depth, heads), out_s...  177 us
    pallas_call x1, Pallas kernels, forward(): pl.pallas_call(functools.partial(forward_kernel, chips, depth, heads), ou...  133 us

commit v1 on v0

--- a/solution.py
+++ b/solution.py
@@ -537,6 +537,7 @@
     out_sem,
     slope_sem,
     att_sem,
+    late_sem,
 ):
     me = Place(chips, depth)
     z, chip, core = me.z, me.chip, me.core
@@ -579,8 +580,8 @@
         def _():
             down_copy(0).start()
 
-    def pass_rest():
-        for h in range(depth - 1):
+    def pass_rest(hops):
+        for h in hops:
 
             @pl.when(z > h)
             def _():
@@ -723,13 +724,43 @@
             me.sibling(),
         )
 
+    def tower_wait(kind):
+        for k in range(1, depth):
+            wz_copy(kind, k).wait_recv()
+
+    def plane_first(kind):
+        for d in range(2):
+            wp_copy(kind, d).start()
+        wc_copy(kind, 0).start()
+
+    def plane_second(kind):
+        for d in range(2):
+            wp_copy(kind, d).wait_recv()
+            wd_copy(kind, d).start()
+            wc_copy(kind, 1 + d).start()
+
+    def plane_last(kind):
+        for d in range(2):
+            wd_copy(kind, d).wait_recv()
+        wc_copy(kind, 3).start()
+        for n in range(chips):
+            wc_copy(kind, n).wait()
+        for d in range(2):
+            wp_copy(kind, d).wait_send()
+            wd_copy(kind, d).wait_send()
+
     def oc_copy():
         spot = owbuf.at[:, core]
         return far_copy(spot, spot, (oc_s, oc_r), 0, me.sibling())
 
-    def cot_copy(k):
+    def cot_copy(n):
+        target = (beside[0], beside[1], across)[n]
         return far_copy(
-            mine(cot_ref, me.chip_at(k)), cbuf.at[chip], (cot_s, cot_r), k - 1, me.plane(k)
+            mine(cot_ref, target),
+            cbuf.at[chip],
+            (cot_s, cot_r),
+            n,
+            (z, target * 2 + core),
         )
 
     keep(mine(cot_ref, chip), cbuf.at[chip])
@@ -749,6 +780,11 @@
             posbuf.at[core, source], posbuf.at[core, source], (posc_s, posc_r), k, me.sibling()
         )
 
+    for k in range(1, depth):
+        wz_copy(1, k).start()
+        for kind in range(3):
+            sends.append(wz_copy(kind, k))
+    pass_rest(range(depth - 2))
     for k in range(chips):
         if k:
             pos_copy(k).wait_recv()
@@ -756,21 +792,21 @@
         for copy in (posc_copy(k), tokc_copy(k)):
             copy.start()
             sends.append(copy)
-    for k in range(1, chips):
-        cot_copy(k).start()
-        sends.append(cot_copy(k))
-    pass_rest()
+    for copy in local[5:]:
+        copy.wait()
+    tower_wait(1)
+    plane_first(1)
+    pass_rest(range(depth - 2, depth - 1))
     for k in range(1, depth):
-        wz_copy(1, k).start()
-        for kind in range(3):
-            sends.append(wz_copy(kind, k))
+        wz_copy(2, k).start()
+    plane_second(1)
+    for n in range(2):
+        cot_copy(n).start()
     for k in range(1, depth):
         vec_copy(k).wait_recv()
     for k in range(chips):
         posc_copy(k).wait_recv()
         tokc_copy(k).wait_recv()
-    for copy in local[5:]:
-        copy.wait()
 
     outs = []
 
@@ -827,54 +863,31 @@
         ]
         return rows
 
-    def tower_wait(kind):
-        for k in range(1, depth):
-            wz_copy(kind, k).wait_recv()
-
-    def plane_first(kind):
-        for d in range(2):
-            wp_copy(kind, d).start()
-        wc_copy(kind, 0).start()
-
-    def plane_second(kind):
-        for d in range(2):
-            wp_copy(kind, d).wait_recv()
-            wd_copy(kind, d).start()
-            wc_copy(kind, 1 + d).start()
-
-    def plane_last(kind):
-        for d in range(2):
-            wd_copy(kind, d).wait_recv()
-        wc_copy(kind, 3).start()
-        for n in range(chips):
-            wc_copy(kind, n).wait()
-        for d in range(2):
-            wp_copy(kind, d).wait_send()
-            wd_copy(kind, d).wait_send()
-
     def hook(i, pair):
         step = i * pairs + pair
         last = per * pairs - 1
 
-        @pl.when(step == min(1, last))
-        def _():
-            tower_wait(1)
-            plane_first(1)
-            for k in range(1, depth):
-                wz_copy(2, k).start()
-
-        @pl.when(step == min(5, last))
+        @pl.when(step == min(2, last))
         def _():
             tower_wait(2)
+            plane_first(2)
             for k in range(1, depth):
                 wz_copy(0, k).start()
 
-        @pl.when(step == min(7, last))
+        @pl.when(step == last)
         def _():
-            plane_second(1)
-            plane_first(2)
+            plane_second(2)
+            cot_copy(2).start()
 
     def attention(qkv, qs, ks, vs, ps, os):
+        def group_copies(i):
+            span = pl.ds(i * pairs, pairs)
+            pieces = ((qs, q_out), (ks, k_out), (vs, v_out), (ps, p_out))
+            return [
+                pltpu.make_async_copy(src.at[span], dst.at[span], att_sem.at[5 + 4 * i + n])
+                for n, (src, dst) in enumerate(pieces)
+            ]
+
         @pl.loop(0, blocks)
         def _(jj):
             x = xbuf[lax.div(jj, chips), lax.rem(jj, chips)].reshape(per * cluster, width)
@@ -917,15 +930,20 @@
                     ctxb[jj // chips, jj % chips, i, :, pl.ds(multiple(pair * 128, 128), 128)] = back
                 hook(i, pair)
 
-        pieces = ((qs, q_out), (ks, k_out), (vs, v_out), (ps, p_out))
-        copies = [
-            pltpu.make_async_copy(src, dst, att_sem.at[n]) for n, (src, dst) in enumerate(pieces)
-        ]
+                @pl.when(pair == pairs - 1)
+                def _():
+                    for copy in group_copies(i):
+                        copy.start()
+
+
         far, own = ctx_copies()
-        for copy in copies + [far, own]:
+        for copy in (far, own):
             copy.start()
-        for copy in copies + [far, own]:
+        for copy in (far, own):
             copy.wait()
+        for i in range(per):
+            for copy in group_copies(i):
+                copy.wait()
 
     def ctx_copies():
         lanes = pl.ds(multiple(core * half, 128), half)
@@ -971,6 +989,13 @@
 
     def feed(hbuf, sbuf):
         step = sbuf.shape[3]
+
+        def late_copies(j):
+            pieces = ((cbuf, lo_out), (n1buf, gr_out), (ctxt, gb_out))
+            return [
+                pltpu.make_async_copy(src.at[j], dst.at[j], late_sem.at[3 * j + n])
+                for n, (src, dst) in enumerate(pieces)
+            ]
 
         def slope_copy(n):
             return pltpu.make_async_copy(
@@ -1003,8 +1028,6 @@
                 hbuf[j, :, lanes] = (pre * cumulative).astype(bf16)
                 sbuf[n % 2, j] = (cumulative + pre * density).astype(bf16)
             slope_copy(n).start()
-            if n == 1:
-                plane_second(2)
 
         emit(vecs, vec_out)
         held = len(outs)
@@ -1015,8 +1038,8 @@
         plane_last(2)
         pass_end()
         emit(rwbuf, rw_out)
-        for k in range(1, chips):
-            cot_copy(k).wait_recv()
+        for n in range(3):
+            cot_copy(n).wait()
         sums[...] = jnp.zeros_like(sums)
         waited = (context_out, outs[held])
         for copy in waited:
@@ -1044,11 +1067,13 @@
             low_grad = grad.astype(bf16)
             sums[2:3, :] += jnp.sum(low_grad.astype(f32), axis=0, keepdims=True)
             ctxt[j] = low_grad.reshape(per, cluster, width)
-
-        emit(cbuf, lo_out)
-        emit(n1buf, gr_out)
-        emit(ctxt, gb_out)
+            for copy in late_copies(j):
+                copy.start()
+
         emit(sums, sum_out)
+        for j in range(chips):
+            for copy in late_copies(j):
+                copy.wait()
         for copy in sends:
             copy.wait_send()
         awc.wait_recv()
@@ -1146,7 +1171,7 @@
             dma((1,)), dma((1,)),
             dma((c,)), dma((c,)),
             dma((1,)), dma((1,)),
-            dma((12,)), dma((24,)), dma((2,)), dma((5,)),
+            dma((12,)), dma((24,)), dma((2,)), dma((5 + 4 * per,)), dma((3 * chips,)),
         ],
         compiler_params=pltpu.CompilerParams(
             collective_id=1, has_side_effects=True, vmem_limit_bytes=63 * 2**20
@@ -1324,12 +1349,9 @@
     posbuf,
     acc,
     gfar,
-    a_mid,
-    a_last,
-    a_done,
-    c_mid,
-    c_last,
-    c_done,
+    p_mid,
+    p_last,
+    p_done,
     o_all,
     o_near,
     o_mid,
@@ -1382,7 +1404,7 @@
     eighth = quarter // blocks
     rows = chips * tile
     me.greet()
-    groups = [sems[n * 10 : (n + 1) * 10] for n in range(5)]
+    groups = [sems[n * 10 : (n + 1) * 10] for n in range(3 + heads // 4)]
     red = Reducer(
         me, r_all.at[core], r_all.at[1 - core], r_near, r_mid, r_last, r_done, groups[0], True
     )
@@ -1608,10 +1630,21 @@
 
     pl.run_scoped(feed_back, vm(shape, bf16))
 
-    def attend_back(qs, ks, vs, ps, xbuf, wbuf, ds, gs, gbuf, tbuf, dw, dwa, dwc):
-        att = Reducer(me, dwa, None, None, a_mid, a_last, a_done, groups[3], False)
-        rest = Reducer(me, dwc, None, None, c_mid, c_last, c_done, groups[4], True)
-        cut = dwa.shape[3]
+    def attend_back(qs, ks, vs, ps, xbuf, wbuf, ds, gs, gbuf, tbuf, dw, dwp):
+        atts = [
+            Reducer(
+                me,
+                dwp.at[n],
+                None,
+                None,
+                p_mid.at[n],
+                p_last.at[n],
+                p_done.at[n],
+                groups[3 + n],
+                n % 2 == 1,
+            )
+            for n in range(pairs)
+        ]
 
         def loads(i, slot):
             span = pl.ds(i * pairs, pairs)
@@ -1747,21 +1780,50 @@
 
         def step_sides():
             red.send_side()
-            out.send_side()
 
         hooks = {}
         steps = [
-            step_out_near,
-            step_exp_mid,
-            step_red_mid,
-            step_exp_last,
-            step_red_last,
-            step_out_last,
-            step_sides,
+            (0, step_out_near),
+            (1, step_exp_mid),
+            (3, step_red_mid),
+            (5, step_exp_last),
+            (6, step_red_last),
+            (7, step_out_last),
+            (8, step_sides),
         ]
-        for n, step in enumerate(steps):
+        for n, step in steps:
             hooks.setdefault(min(n, per * pairs - 1), []).append(step)
-
+        depth_rows = quarter // chips
+
+        def pair_grad(n, slot):
+            lanes = [slice(p * half + n * 128, p * half + (n + 1) * 128) for p in range(3)]
+            total = jnp.concatenate([dw[:, lane] for lane in lanes], axis=1)
+            line = jnp.zeros((1, 384), f32)
+            for b in range(2):
+                x = jnp.concatenate([xbuf[b, j] for j in range(chips)], axis=0)
+                g = jnp.concatenate(
+                    [
+                        jnp.concatenate([gbuf[slot, b, j, :, lane] for lane in lanes], axis=1)
+                        for j in range(chips)
+                    ],
+                    axis=0,
+                )
+                total = total + dot_first(x, g)
+                line = line + jnp.sum(g.astype(f32), axis=0, keepdims=True)
+            for p, lane in enumerate(lanes):
+                bbuf[0:1, lane] += line[:, p * 128 : (p + 1) * 128]
+            low = total.astype(bf16)
+            for a in range(depth):
+                for b in range(chips):
+                    begin = (a * chips + b) * depth_rows
+                    piece = low[begin : begin + depth_rows]
+                    if atts[n].tower_first:
+                        dwp[n, a, b] = piece
+                    else:
+                        dwp[n, b, a] = piece
+            atts[n].send_mid()
+
+        dw[...] = jnp.zeros_like(dw)
         for i in range(per):
             slot = i % 2
             for copy in loads(i, slot):
@@ -1773,16 +1835,20 @@
             if i + 1 < per:
                 for copy in loads(i + 1, 1 - slot):
                     copy.start()
+            if i == per - 1:
+                load_x(i).wait()
 
             @pl.loop(0, pairs)
             def _(pair):
                 clusters(i, slot, pair)
                 for n in range(pairs):
-                    if hooks.get(i * pairs + n):
+                    if hooks.get(i * pairs + n) or i == per - 1:
 
                         @pl.when(pair == n)
                         def _():
-                            for step in hooks[i * pairs + n]:
+                            if i == per - 1:
+                                pair_grad(n, slot)
+                            for step in hooks.get(i * pairs + n, ()):
                                 step()
 
             if i >= 2:
@@ -1790,66 +1856,56 @@
                 for k in range(1, chips):
                     token_copy(i - 2, slot, k).wait()
             give(slot).start()
-            load_x(i).wait()
-            for b in range(2):
-                x = jnp.concatenate([xbuf[b, j] for j in range(chips)], axis=0)
-                g = jnp.concatenate([gbuf[slot, b, j] for j in range(chips)], axis=0)
-                term = dot_first(x, g)
-                if i == 0 and b == 0:
-                    dw[...] = term
-                else:
-                    dw[...] += term
-                bbuf[0:1, :] += jnp.sum(g.astype(f32), axis=0, keepdims=True)
             if i + 1 < per:
+                load_x(i).wait()
+                for b in range(2):
+                    x = jnp.concatenate([xbuf[b, j] for j in range(chips)], axis=0)
+                    g = jnp.concatenate([gbuf[slot, b, j] for j in range(chips)], axis=0)
+                    dw[...] += dot_first(x, g)
+                    bbuf[0:1, :] += jnp.sum(g.astype(f32), axis=0, keepdims=True)
                 load_x(i + 1).start()
 
-        depth_rows = quarter // chips
-        for a in range(depth):
-            for b in range(chips):
-                begin = (a * chips + b) * depth_rows
-                dwa[b, a] = dw[begin : begin + depth_rows, :cut].astype(bf16)
-                dwc[a, b] = dw[begin : begin + depth_rows, cut:].astype(bf16)
-        att.send_mid()
-        rest.send_mid()
         biases.send(1)
         token_rows(per - 1, (per - 1) % 2)
         emit(vbuf, vec_out)
+        out.send_side()
+        for n in range(pairs - 1):
+            atts[n].fold_mid()
+            atts[n].send_last()
+        biases.fold(1)
+        biases.send(2)
         exp.finish()
         for c in range(2):
             for p in range(chips):
                 emit(e_done.at[c, p], ew_out.at[:, pl.ds((c * chips + p) * wide, wide)])
+        for n in range(pairs - 1, pairs):
+            atts[n].fold_mid()
+            atts[n].send_last()
+        for n in range(pairs - 1):
+            atts[n].fold_last()
+            atts[n].send_back()
         red.finish()
         for c in range(2):
             emit(r_done.at[c], rw_out.at[:, :, pl.ds(c * wide, wide)])
         out.finish()
         emit(o_done, ow_out)
-        biases.fold(1)
-        biases.send(2)
-        att.fold_mid()
-        att.send_last()
-        rest.fold_mid()
-        rest.send_last()
         biases.fold(2)
         share_bias = far_copy(bbuf, bias_out.at[core], (b_s, b_r), 0, me.sibling())
         share_bias.start()
         emit(bbuf, bias_out.at[core])
-        att.fold_last()
-        att.send_back()
-        rest.fold_last()
-        rest.send_back()
-        att.send_side()
-        rest.send_side()
-        for reducer, done, begin in ((att, a_done, 0), (rest, c_done, cut)):
-            reducer.finish()
-            end = begin + done.shape[3]
-            for part in range(3):
-                lo, hi = max(begin, part * half), min(end, (part + 1) * half)
-                for c in range(2):
-                    if lo < hi:
-                        emit(
-                            done.at[c, :, :, pl.ds(lo - begin, hi - lo)],
-                            aw_out.at[:, :, pl.ds((part + c) * half + lo, hi - lo)],
-                        )
+        for n in range(pairs - 1, pairs):
+            atts[n].fold_last()
+            atts[n].send_back()
+        for n in range(pairs):
+            atts[n].send_side()
+        for n in range(pairs):
+            atts[n].finish()
+            for c in range(2):
+                for part in range(3):
+                    emit(
+                        p_done.at[n, c, :, :, pl.ds(part * 128, 128)],
+                        aw_out.at[:, :, pl.ds((2 * part + c) * half + n * 128, 128)],
+                    )
         for i in range(max(per - 2, 0), per):
             token_keep(i, i % 2).wait()
             for k in range(1, chips):
@@ -1875,8 +1931,7 @@
         vm((2, 2, chips, cluster, 3 * half), bf16),
         vm((2, chips, cluster, width), bf16),
         vm((width, 3 * half), f32),
-        vm((chips, depth, quarter // chips, a_mid.shape[3]), bf16),
-        vm((depth, chips, quarter // chips, c_mid.shape[3]), bf16),
+        vm((pairs, depth, chips, quarter // chips, 384), bf16),
     )
 
 
@@ -1890,7 +1945,7 @@
     eighth, strip, wide = quarter // blocks, width // chips, hidden // blocks
     rows = quarter // chips
     c, t = chips - 1, depth - 1
-    cut = 3 * half // 128 * 5 // 9 * 128
+    pairs = heads // 4
     shapes = [
         ((chips * per, cluster, width), bf16),
         ((chips * per, cluster, width), bf16),
@@ -1922,12 +1977,9 @@
             vm(arrays[4].shape, jnp.int32),
             vm((chips, per * cluster, width), f32),
             vm((2, chips, cluster, 3 * half), bf16),
-            vm((c, depth, rows, cut), bf16),
-            vm((t, rows, cut), bf16),
-            vm((2, chips, rows, cut), bf16),
-            vm((t, chips, rows, 3 * half - cut), bf16),
-            vm((c, rows, 3 * half - cut), bf16),
-            vm((2, chips, rows, 3 * half - cut), bf16),
+            vm((pairs, t, chips, rows, 384), bf16),
+            vm((pairs, t, rows, 384), bf16),
+            vm((pairs, 2, chips, rows, 384), bf16),
             vm((2, chips, depth, eighth, width), bf16),
             vm((chips, depth, eighth, width), bf16),
             vm((c, depth, eighth, width), bf16),
@@ -1951,13 +2003,12 @@
             dma((chips,)), dma((chips,)), dma((2,)), dma((2,)),
             dma((per * c,)), dma((per * c,)),
             dma((c,)), dma((c,)),
-            dma((19,)), dma((1 + per + 16 + blocks,)),
+            dma((19,)), dma((1 + per + 6 + blocks + 6 * pairs,)),
             dma((chips + t,)), dma((chips + t,)), dma((chips + t,)), dma((chips + t,)),
             *reducing(depth, t, c),
             *reducing(chips, c, t),
             *reducing(chips, c, t),
-            *reducing(1, c, t),
-            *reducing(1, t, c),
+            *[sem for n in range(pairs) for sem in reducing(1, c, t)],
         ],
         compiler_params=pltpu.CompilerParams(
             collective_id=2, has_side_effects=True, vmem_limit_bytes=63 * 2**20

time: 334 us -> 317 us (0.949)
  Pallas kernels: 310 us -> 292 us
    pallas_call x1, Pallas kernels: 177 us -> 161 us  [back(): pl.pallas_call(functools.partial(back_kernel, chips, depth, heads), out_s...]
where the time goes in v1:
time: 317 us; the launch traced here: 311 us
  Pallas kernels  292 us (92%)
  local copies, waits for them, and re-layouts  10.3 us (3%)
  other arithmetic  7.86 us (2%)
    pallas_call x1, Pallas kernels, back(): pl.pallas_call(functools.partial(back_kernel, chips, depth, heads), out_s...  161 us
    pallas_call x1, Pallas kernels, forward(): pl.pallas_call(functools.partial(forward_kernel, chips, depth, heads), ou...  131 us

profile of v1, /device:TPU:0, one launch (start us, length us, event | category | flops | bytes accessed | tf_op | source)
XLA Modules:
  0.0 311.5 jit_solution(14122365849447427012)
XLA Ops:
  0.6 0.9 fusion.10
  1.6 0.8 convert_add_fusion
  2.3 0.6 reshape.132.vec_ref
  3.0 1.0 add_select_fusion
  4.0 0.6 fusion.1
  4.6 0.7 convert_element_type.81.pos_ref
  5.3 130.8 %forward.1 = (bf16[2,4,3,128,768]{4,3,2,1,0:T(8,128)(2,1)}, bf16[4,3,128,768]{3,2,1,0:T(8,128)(2,1)}, bf16[9,8,128,128]{3,2,1,0:T(8,128)(2,1)}, bf16[9,8,128,128...) custom-call(bf16[12,128,768]{2,1,0:T(8,128)(2,1)} %tok_ref.1, ...), custom_call_target="tpu_custom_call" | custom-call | tf_op jit(solution)/shard_map/forward/pallas_call | solution.py:1141
  136.1 161.0 %back.1 = (bf16[12,128,768]{2,1,0:T(8,128)(2,1)}, bf16[12,128,768]{2,1,0:T(8,128)(2,1)}, bf16[4,48,2304]{2,1,0:T(8,128)(2,1)}, bf16[2,4,24,768]{3,2,1,0:T(8,128)...) custom-call(bf16[9,8,128,128]{3,2,1,0:T(8,128)(2,1)} %get-tuple-elem, ...), custom_call_target="tpu_custom_call" | custom-call | tf_op jit(solution)/shard_map/back/pallas_call | solution.py:1970
  297.1 0.8 slice_reduce_fusion.1
  298.0 0.7 slice.56
  298.7 0.7 fusion.8
  299.4 1.4 bitcast_convert_fusion
  300.8 0.0 copy-start.2
  300.8 2.0 copy.33
  302.8 0.0 copy-start.3
  302.8 0.0 copy-done.2
  302.8 0.0 copy-start.4
  302.8 1.7 convert_element_type.86
  304.5 0.0 copy-start.5
  304.5 0.0 copy-start.1
  304.5 0.0 copy-done.3
  304.5 1.4 bitcast_convert_fusion.1
  305.8 0.0 copy-done.4
  305.8 0.9 bitcast_convert_fusion.2
  306.7 0.0 copy-done.5
  306.7 0.6 dynamic-slice_reduce_fusion
  307.3 0.0 copy-done.1
  307.3 0.0 copy-start
  307.3 1.4 copy.37
  308.7 1.1 copy-done
  309.9 1.4 copy.38
  (5 shorter events, 0.0 us)
Async XLA Ops:
  300.8 2.0 copy-start.2
  302.8 1.7 copy-start.3
  302.8 3.1 copy-start.4
  304.5 2.3 copy-start.5
  304.5 2.9 copy-start.1
  307.3 2.5 copy-start

commit v2 on v1

--- a/solution.py
+++ b/solution.py
@@ -1038,7 +1038,7 @@
         plane_last(2)
         pass_end()
         emit(rwbuf, rw_out)
-        for n in range(3):
+        for n in range(2):
             cot_copy(n).wait()
         sums[...] = jnp.zeros_like(sums)
         waited = (context_out, outs[held])
@@ -1046,7 +1046,14 @@
             copy.wait()
 
         @pl.loop(0, chips)
-        def _(j):
+        def _(n):
+            j = 2 * lax.rem(lax.div(chip, 2) + lax.div(n, 2), 2)
+            j = j + lax.rem(chip + n, 2)
+
+            @pl.when(n == chips - 1)
+            def _():
+                cot_copy(2).wait()
+
             branch = vec(5)
             for zz in range(depth):
                 span = hidden // depth
@@ -1439,7 +1446,7 @@
     def order(n):
         return lax.rem(n + z + chip, counts)
 
-    def fold(n):
+    def fold_red(n):
         at = order(n)
         red.fold_near(at)
         k = lax.rem(at - z + depth, depth)
@@ -1447,6 +1454,9 @@
         @pl.when(k != 0)
         def _():
             red.mid_copy(k).start()
+
+    def fold_exp(n):
+        at = order(n)
 
         @pl.when(lax.div(at, 2) == core)
         def _():
@@ -1507,6 +1517,17 @@
                 for copy in chunk(n + 1, 1 - slot):
                     copy.start()
 
+            term = dot_rows(gbt[...], hid[slot].reshape(rows, block)).astype(bf16)
+            for side in range(2):
+                r_all[side, at] = term[:, side * wide : (side + 1) * wide].reshape(
+                    chips, strip, wide
+                )
+            red.near_copy(at).start()
+
+            @pl.when(n > 0)
+            def _():
+                fold_exp(n - 1)
+
             up = rwc[slot].reshape(block, width)
             down = ewc[slot].reshape(width, block)
             total = jnp.zeros((1, block), f32)
@@ -1517,12 +1538,7 @@
                 acc[j] += dot_lanes(low, down)
                 total = total + jnp.sum(low.astype(f32), axis=0, keepdims=True)
             vbuf[pl.ds(8 + at, 1), :block] = total
-            term = dot_rows(gbt[...], hid[slot].reshape(rows, block)).astype(bf16)
-            for side in range(2):
-                r_all[side, at] = term[:, side * wide : (side + 1) * wide].reshape(
-                    chips, strip, wide
-                )
-            red.near_copy(at).start()
+            fold_red(n)
             term = dot_rows(mlt[...], gpb[...].reshape(rows, block)).astype(bf16)
             for side in range(2):
                 e_all[lax.div(at, 2), lax.rem(at, 2) * 2 + side] = term[
@@ -1533,10 +1549,6 @@
             def _():
                 for side in range(2):
                     exp.near_copy(lax.rem(at, 2) * 2 + side).start()
-
-            @pl.when(n > 0)
-            def _():
-                fold(n - 1)
 
     def first_norm(gb, n1, inv, ctx, ow, dsnd):
         later = [
@@ -1553,7 +1565,7 @@
         n1_copy(0).start()
         for copy in later:
             copy.start()
-        fold(counts - 1)
+        fold_exp(counts - 1)
         for copy in later:
             copy.wait()
         gain = vecs[3:4, :]
@@ -1630,7 +1642,7 @@
 
     pl.run_scoped(feed_back, vm(shape, bf16))
 
-    def attend_back(qs, ks, vs, ps, xbuf, wbuf, ds, gs, gbuf, tbuf, dw, dwp):
+    def attend_back(qs, ks, vs, ps, xbuf, wbuf, ds, gs, gbuf, tbuf, dw, dwp, turned):
         atts = [
             Reducer(
                 me,
@@ -1886,7 +1898,8 @@
             atts[n].send_back()
         red.finish()
         for c in range(2):
-            emit(r_done.at[c], rw_out.at[:, :, pl.ds(c * wide, wide)])
+            turned[c] = jnp.transpose(r_done[c].reshape(width, wide))
+            emit(turned.at[c], rw_out.at[c])
         out.finish()
         emit(o_done, ow_out)
         biases.fold(2)
@@ -1932,6 +1945,7 @@
         vm((2, chips, cluster, width), bf16),
         vm((width, 3 * half), f32),
         vm((pairs, depth, chips, quarter // chips, 384), bf16),
+        vm((2, wide, width), bf16),
     )
 
 
@@ -1952,7 +1966,7 @@
         ((chips, rows, 3 * width), bf16),
         ((2, chips, eighth, width), bf16),
         ((quarter, hidden), bf16),
-        ((chips, strip, 2 * wide), bf16),
+        ((2, wide, width), bf16),
         ((8 + blocks, width), f32),
         ((2, 8, 3 * half), f32),
     ]
@@ -2161,7 +2175,7 @@
         six[4],
         ew_grad.astype(f32),
         up,
-        jnp.transpose(rw_grad.reshape(width, -1)).astype(f32),
+        rw_grad.reshape(-1, width).astype(f32),
         six[2],
         six[0],
         six[1],

time: 317 us -> 308 us (0.972)
  Pallas kernels: 292 us -> 285 us
    pallas_call x1, Pallas kernels: 161 us -> 154 us  [back(): pl.pallas_call(functools.partial(back_kernel, chips, depth, heads), out_s...]
where the time goes in v2:
time: 308 us; the launch traced here: 304 us
  Pallas kernels  285 us (93%)
  other arithmetic  9.27 us (3%)
  local copies, waits for them, and re-layouts  8.41 us (3%)
    pallas_call x1, Pallas kernels, back(): pl.pallas_call(functools.partial(back_kernel, chips, depth, heads), out_s...  154 us
    pallas_call x1, Pallas kernels, forward(): pl.pallas_call(functools.partial(forward_kernel, chips, depth, heads), ou...  131 us

profile of v2, /device:TPU:0, one launch (start us, length us, event | category | flops | bytes accessed | tf_op | source)
XLA Modules:
  0.0 304.4 jit_solution(12509826700066102657)
XLA Ops:
  0.6 0.9 fusion.10
  1.6 0.8 convert_add_fusion
  2.3 0.6 reshape.132.vec_ref
  3.0 1.0 add_select_fusion
  4.0 0.6 fusion.1
  4.6 0.7 convert_element_type.78.pos_ref
  5.3 130.8 %forward.1 = (bf16[2,4,3,128,768]{4,3,2,1,0:T(8,128)(2,1)}, bf16[4,3,128,768]{3,2,1,0:T(8,128)(2,1)}, bf16[9,8,128,128]{3,2,1,0:T(8,128)(2,1)}, bf16[9,8,128,128...) custom-call(bf16[12,128,768]{2,1,0:T(8,128)(2,1)} %tok_ref.1, ...), custom_call_target="tpu_custom_call" | custom-call | tf_op jit(solution)/shard_map/forward/pallas_call | solution.py:1148
  136.1 154.4 %back.1 = (bf16[12,128,768]{2,1,0:T(8,128)(2,1)}, bf16[12,128,768]{2,1,0:T(8,128)(2,1)}, bf16[4,48,2304]{2,1,0:T(8,128)(2,1)}, bf16[2,4,24,768]{3,2,1,0:T(8,128)...) custom-call(bf16[9,8,128,128]{3,2,1,0:T(8,128)(2,1)} %get-tuple-elem, ...), custom_call_target="tpu_custom_call" | custom-call | tf_op jit(solution)/shard_map/back/pallas_call | solution.py:1984
  290.5 0.0 copy-start.2
  290.5 0.9 slice_reduce_fusion.1
  291.5 0.7 slice.56
  292.2 0.7 fusion.8
  292.9 2.8 bitcast_convert_fusion
  295.7 0.0 copy-start.3
  295.7 0.0 copy-done.2
  295.7 0.0 copy-start.4
  295.7 1.7 convert_element_type.83
  297.4 0.0 copy-start.5
  297.4 0.0 copy-start.1
  297.4 0.0 copy-done.3
  297.4 1.4 bitcast_convert_fusion.1
  298.8 0.0 copy-done.4
  298.8 0.9 bitcast_convert_fusion.2
  299.7 0.0 copy-done.5
  299.7 0.6 dynamic-slice_reduce_fusion
  300.3 0.0 copy-done.1
  300.3 0.0 copy-start
  300.3 1.4 copy.35
  301.7 1.1 copy-done
  302.8 1.4 copy.36
  (5 shorter events, 0.0 us)
Async XLA Ops:
  290.5 5.2 %copy-start.2 = (bf16[192,3072]{1,0:T(8,128)(2,1)S(1)}, bf16[192,3072]{1,0:T(8,128)(2,1)}, u32[]{:S(2)}) copy-start(bf16[192,3072]{1,0:T(8,128)(2,1)} %get-tuple-element.71) | copy-start | bytes 3538948
  295.7 1.7 copy-start.3
  295.7 3.1 %copy-start.4 = (bf16[2,4,24,768]{3,2,1,0:T(8,128)(2,1)S(1)}, bf16[2,4,24,768]{3,2,1,0:T(8,128)(2,1)}, u32[]{:S(2)}) copy-start(bf16[2,4,24,768]{3,2,1,0:T(8,128)(2,1)} %get-tuple-element.69) | copy-start | bytes 884740
  297.4 2.3 copy-start.5
  297.4 2.9 copy-start.1
  300.3 2.5 copy-start

commit v3 on v2

--- a/solution.py
+++ b/solution.py
@@ -877,7 +877,6 @@
         @pl.when(step == last)
         def _():
             plane_second(2)
-            cot_copy(2).start()
 
     def attention(qkv, qs, ks, vs, ps, os):
         def group_copies(i):
@@ -1014,6 +1013,7 @@
             invbuf[j] = jnp.broadcast_to(inverse, (tile, 128))
             mlbuf[j] = (normed * vec(3) + vec(4)).astype(bf16).reshape(per, cluster, width)
 
+        cot_copy(2).start()
         plane_last(1)
         emit(ewbuf, ew_out)
         for n in range(hidden // step):
@@ -1490,20 +1490,21 @@
             fetch(late_ref, vbuf.at[pl.ds(0, 8)], 12),
             fetch(pos_ref, posbuf, 18),
         ]
-        for copy in begin + chunk(0, 0) + later:
+        for copy in begin[:1] + chunk(0, 0) + begin[1:] + later:
             copy.start()
         for k in range(1, chips):
             lo_copy(k).start()
         lo_keep.start()
         vbuf[8:, :] = jnp.zeros((blocks, width), f32)
-        for copy in begin:
-            copy.wait()
+        begin[0].wait()
         for j in range(chips):
-            span = slice(j * tile, (j + 1) * tile)
-            mlt[:, span] = jnp.transpose(gpb[j].reshape(tile, width))
-            gbt[:, span] = jnp.transpose(gb[j].reshape(tile, width))
-        for copy in later:
-            copy.wait()
+            gbt[:, j * tile : (j + 1) * tile] = jnp.transpose(gb[j].reshape(tile, width))
+
+        def settle():
+            for copy in begin[1:] + later:
+                copy.wait()
+            for j in range(chips):
+                mlt[:, j * tile : (j + 1) * tile] = jnp.transpose(gpb[j].reshape(tile, width))
 
         @pl.loop(0, counts)
         def _(n):
@@ -1523,6 +1524,10 @@
                     chips, strip, wide
                 )
             red.near_copy(at).start()
+
+            @pl.when(n == 0)
+            def _():
+                settle()
 
             @pl.when(n > 0)
             def _():
@@ -1739,11 +1744,10 @@
 
         def token_rows(i, slot):
             give(slot).wait()
-            for j in range(chips):
-                near = dot_lanes(gbuf[slot, core, j], wbuf[core])
-                distant = dot_lanes(gfar[slot, j], wbuf[1 - core])
-                resid = acc[j, i * cluster : (i + 1) * cluster, :]
-                tbuf[slot, j] = (resid + near + distant).astype(bf16)
+            near = dot_lanes(gbuf[slot, core].reshape(chips * cluster, 3 * half), wbuf[core])
+            distant = dot_lanes(gfar[slot].reshape(chips * cluster, 3 * half), wbuf[1 - core])
+            resid = acc[:, i * cluster : (i + 1) * cluster, :].reshape(chips * cluster, width)
+            tbuf[slot] = (resid + near + distant).astype(bf16).reshape(chips, cluster, width)
             token_keep(i, slot).start()
             for k in range(1, chips):
                 token_copy(i, slot, k).start()

time: 308 us -> 305 us (level)
  Pallas kernels: 285 us -> 281 us
    pallas_call x1, Pallas kernels: 154 us -> 151 us  [back(): pl.pallas_call(functools.partial(back_kernel, chips, depth, heads), out_s...]
where the time goes in v3:
time: 305 us; the launch traced here: 301 us
  Pallas kernels  281 us (92%)
  other arithmetic  9.27 us (3%)
  local copies, waits for them, and re-layouts  8.41 us (3%)
    pallas_call x1, Pallas kernels, back(): pl.pallas_call(functools.partial(back_kernel, chips, depth, heads), out_s...  151 us
    pallas_call x1, Pallas kernels, forward(): pl.pallas_call(functools.partial(forward_kernel, chips, depth, heads), ou...  131 us

profile of v3, /device:TPU:0, one launch (start us, length us, event | category | flops | bytes accessed | tf_op | source)
XLA Modules:
  0.0 300.7 jit_solution(4299777803812422333)
XLA Ops:
  0.6 0.9 fusion.10
  1.6 0.8 convert_add_fusion
  2.3 0.6 reshape.132.vec_ref
  3.0 1.0 add_select_fusion
  4.0 0.6 fusion.1
  4.6 0.7 convert_element_type.78.pos_ref
  5.3 130.8 %forward.1 = (bf16[2,4,3,128,768]{4,3,2,1,0:T(8,128)(2,1)}, bf16[4,3,128,768]{3,2,1,0:T(8,128)(2,1)}, bf16[9,8,128,128]{3,2,1,0:T(8,128)(2,1)}, bf16[9,8,128,128...) custom-call(bf16[12,128,768]{2,1,0:T(8,128)(2,1)} %tok_ref.1, ...), custom_call_target="tpu_custom_call" | custom-call | tf_op jit(solution)/shard_map/forward/pallas_call | solution.py:1148
  136.1 150.6 %back.1 = (bf16[12,128,768]{2,1,0:T(8,128)(2,1)}, bf16[12,128,768]{2,1,0:T(8,128)(2,1)}, bf16[4,48,2304]{2,1,0:T(8,128)(2,1)}, bf16[2,4,24,768]{3,2,1,0:T(8,128)...) custom-call(bf16[9,8,128,128]{3,2,1,0:T(8,128)(2,1)} %get-tuple-elem, ...), custom_call_target="tpu_custom_call" | custom-call | tf_op jit(solution)/shard_map/back/pallas_call | solution.py:1988
  286.7 0.0 copy-start.2
  286.7 0.9 slice_reduce_fusion.1
  287.7 0.7 slice.56
  288.4 0.7 fusion.8
  289.1 2.8 bitcast_convert_fusion
  291.9 0.0 copy-start.3
  291.9 0.0 copy-done.2
  291.9 0.0 copy-start.4
  291.9 1.7 convert_element_type.83
  293.6 0.0 copy-start.5
  293.6 0.0 copy-start.1
  293.6 0.0 copy-done.3
  293.6 1.4 bitcast_convert_fusion.1
  295.0 0.0 copy-done.4
  295.0 0.9 bitcast_convert_fusion.2
  295.9 0.0 copy-done.5
  295.9 0.6 dynamic-slice_reduce_fusion
  296.5 0.0 copy-done.1
  296.5 0.0 copy-start
  296.5 1.4 copy.35
  297.9 1.1 copy-done
  299.0 1.4 copy.36
  (5 shorter events, 0.0 us)
Async XLA Ops:
  286.7 5.2 %copy-start.2 = (bf16[192,3072]{1,0:T(8,128)(2,1)S(1)}, bf16[192,3072]{1,0:T(8,128)(2,1)}, u32[]{:S(2)}) copy-start(bf16[192,3072]{1,0:T(8,128)(2,1)} %get-tuple-element.71) | copy-start | bytes 3538948
  291.9 1.7 copy-start.3
  291.9 3.1 %copy-start.4 = (bf16[2,4,24,768]{3,2,1,0:T(8,128)(2,1)S(1)}, bf16[2,4,24,768]{3,2,1,0:T(8,128)(2,1)}, u32[]{:S(2)}) copy-start(bf16[2,4,24,768]{3,2,1,0:T(8,128)(2,1)} %get-tuple-element.69) | copy-start | bytes 884740
  293.6 2.3 copy-start.5
  293.6 2.9 copy-start.1
  296.5 2.5 copy-start

commit v4 on v3

--- a/solution.py
+++ b/solution.py
@@ -483,7 +483,6 @@
     hid_out,
     slope_out,
     lo_out,
-    gr_out,
     gb_out,
     sum_out,
     xbuf,
@@ -990,9 +989,9 @@
         step = sbuf.shape[3]
 
         def late_copies(j):
-            pieces = ((cbuf, lo_out), (n1buf, gr_out), (ctxt, gb_out))
+            pieces = ((cbuf, lo_out), (ctxt, gb_out))
             return [
-                pltpu.make_async_copy(src.at[j], dst.at[j], late_sem.at[3 * j + n])
+                pltpu.make_async_copy(src.at[j], dst.at[j], late_sem.at[2 * j + n])
                 for n, (src, dst) in enumerate(pieces)
             ]
 
@@ -1030,7 +1029,6 @@
             slope_copy(n).start()
 
         emit(vecs, vec_out)
-        held = len(outs)
         emit(n1buf, n1_out)
         emit(invbuf, inv_out)
         emit(mlbuf, ml_out)
@@ -1041,7 +1039,7 @@
         for n in range(2):
             cot_copy(n).wait()
         sums[...] = jnp.zeros_like(sums)
-        waited = (context_out, outs[held])
+        waited = (context_out,)
         for copy in waited:
             copy.wait()
 
@@ -1070,7 +1068,6 @@
             first = jnp.mean(scaled, axis=1, keepdims=True)
             second = jnp.mean(scaled * normed, axis=1, keepdims=True)
             grad = inverse * (scaled - first - normed * second)
-            n1buf[j] = grad
             low_grad = grad.astype(bf16)
             sums[2:3, :] += jnp.sum(low_grad.astype(f32), axis=0, keepdims=True)
             ctxt[j] = low_grad.reshape(per, cluster, width)
@@ -1139,7 +1136,6 @@
         ((chips, tile, hidden), bf16),
         ((chips, tile, hidden), bf16),
         ((chips, per, cluster, width), bf16),
-        ((chips, tile, width), f32),
         ((chips, per, cluster, width), bf16),
         ((8, width), f32),
     ]
@@ -1178,7 +1174,7 @@
             dma((1,)), dma((1,)),
             dma((c,)), dma((c,)),
             dma((1,)), dma((1,)),
-            dma((12,)), dma((24,)), dma((2,)), dma((5 + 4 * per,)), dma((3 * chips,)),
+            dma((12,)), dma((24,)), dma((2,)), dma((5 + 4 * per,)), dma((2 * chips,)),
         ],
         compiler_params=pltpu.CompilerParams(
             collective_id=1, has_side_effects=True, vmem_limit_bytes=63 * 2**20
@@ -1341,7 +1337,6 @@
     hid_ref,
     slope_ref,
     lo_ref,
-    gr_ref,
     gb_ref,
     late_ref,
     token_out,
@@ -1483,7 +1478,6 @@
         begin = [
             fetch(gb_ref, gb, 8),
             fetch(ml_ref, gpb, 9),
-            fetch(gr_ref, acc, 10),
         ]
         later = [
             fetch(vec_ref, vecs, 11),
@@ -1505,6 +1499,7 @@
                 copy.wait()
             for j in range(chips):
                 mlt[:, j * tile : (j + 1) * tile] = jnp.transpose(gpb[j].reshape(tile, width))
+                acc[j] = gb[j].reshape(tile, width).astype(f32)
 
         @pl.loop(0, counts)
         def _(n):
@@ -2118,7 +2113,6 @@
         hidden,
         slope,
         layer_out,
-        grad_resid_two,
         grad_branch_two,
         late_sums,
     ) = forward(
@@ -2154,7 +2148,6 @@
             hidden,
             slope,
             layer_out,
-            grad_resid_two,
             grad_branch_two,
             late_sums,
         ),

time: 305 us -> 303 us (level)
  no operation moved by 1% of the time
where the time goes in v4:
time: 303 us; the launch traced here: 299 us
  Pallas kernels  280 us (92%)
  other arithmetic  9.27 us (3%)
  local copies, waits for them, and re-layouts  8.41 us (3%)
    pallas_call x1, Pallas kernels, back(): pl.pallas_call(functools.partial(back_kernel, chips, depth, heads), out_s...  151 us
    pallas_call x1, Pallas kernels, forward(): pl.pallas_call(functools.partial(forward_kernel, chips, depth, heads), ou...  129 us

profile of v4, /device:TPU:0, one launch (start us, length us, event | category | flops | bytes accessed | tf_op | source)
XLA Modules:
  0.0 299.3 jit_solution(9697811141362743570)
XLA Ops:
  0.6 0.9 fusion.10
  1.6 0.8 convert_add_fusion
  2.3 0.6 reshape.132.vec_ref
  3.0 1.0 add_select_fusion
  4.0 0.6 fusion.1
  4.6 0.7 convert_element_type.78.pos_ref
  5.3 129.3 %forward.1 = (bf16[2,4,3,128,768]{4,3,2,1,0:T(8,128)(2,1)}, bf16[4,3,128,768]{3,2,1,0:T(8,128)(2,1)}, bf16[9,8,128,128]{3,2,1,0:T(8,128)(2,1)}, bf16[9,8,128,128...) custom-call(bf16[12,128,768]{2,1,0:T(8,128)(2,1)} %tok_ref.1, ...), custom_call_target="tpu_custom_call" | custom-call | tf_op jit(solution)/shard_map/forward/pallas_call | solution.py:1144
  134.6 150.7 %back.1 = (bf16[12,128,768]{2,1,0:T(8,128)(2,1)}, bf16[12,128,768]{2,1,0:T(8,128)(2,1)}, bf16[4,48,2304]{2,1,0:T(8,128)(2,1)}, bf16[2,4,24,768]{3,2,1,0:T(8,128)...) custom-call(bf16[9,8,128,128]{3,2,1,0:T(8,128)(2,1)} %get-tuple-elem, ...), custom_call_target="tpu_custom_call" | custom-call | tf_op jit(solution)/shard_map/back/pallas_call | solution.py:1983
  285.3 0.0 copy-start.2
  285.3 0.9 slice_reduce_fusion.1
  286.3 0.7 slice.56
  287.0 0.7 fusion.8
  287.7 2.8 bitcast_convert_fusion
  290.5 0.0 copy-start.3
  290.5 0.0 copy-done.2
  290.5 0.0 copy-start.4
  290.5 1.7 convert_element_type.83
  292.2 0.0 copy-start.5
  292.2 0.0 copy-start.1
  292.2 0.0 copy-done.3
  292.2 1.4 bitcast_convert_fusion.1
  293.6 0.0 copy-done.4
  293.6 0.9 bitcast_convert_fusion.2
  294.5 0.0 copy-done.5
  294.5 0.6 dynamic-slice_reduce_fusion
  295.1 0.0 copy-done.1
  295.1 0.0 copy-start
  295.1 1.4 copy.35
  296.5 1.1 copy-done
  297.6 1.4 copy.36
  (5 shorter events, 0.0 us)
Async XLA Ops:
  285.3 5.2 %copy-start.2 = (bf16[192,3072]{1,0:T(8,128)(2,1)S(1)}, bf16[192,3072]{1,0:T(8,128)(2,1)}, u32[]{:S(2)}) copy-start(bf16[192,3072]{1,0:T(8,128)(2,1)} %get-tuple-element.69) | copy-start | bytes 3538948
  290.5 1.7 copy-start.3
  290.5 3.1 %copy-start.4 = (bf16[2,4,24,768]{3,2,1,0:T(8,128)(2,1)S(1)}, bf16[2,4,24,768]{3,2,1,0:T(8,128)(2,1)}, u32[]{:S(2)}) copy-start(bf16[2,4,24,768]{3,2,1,0:T(8,128)(2,1)} %get-tuple-element.67) | copy-start | bytes 884740
  292.2 2.3 copy-start.5
  292.2 2.9 copy-start.1
  295.1 2.5 copy-start

commit v5 on v4

--- a/solution.py
+++ b/solution.py
@@ -1002,8 +1002,7 @@
                 slope_sem.at[n % 2],
             )
 
-        @pl.loop(0, chips)
-        def _(j):
+        for j in range(chips):
             rows = ctxt[j].reshape(tile, width)
             branch = dot_rows(rows, owbuf[...].reshape(width, width))
             resid = xbuf[core, j].reshape(tile, width).astype(f32) + branch + vec(2)
@@ -1043,13 +1042,11 @@
         for copy in waited:
             copy.wait()
 
-        @pl.loop(0, chips)
-        def _(n):
-            j = 2 * lax.rem(lax.div(chip, 2) + lax.div(n, 2), 2)
+        for n in range(chips):
+            j = 2 * lax.rem(lax.div(chip, 2) + n // 2, 2)
             j = j + lax.rem(chip + n, 2)
 
-            @pl.when(n == chips - 1)
-            def _():
+            if n == chips - 1:
                 cot_copy(2).wait()
 
             branch = vec(5)
@@ -1839,7 +1836,7 @@
             slot = i % 2
             for copy in loads(i, slot):
                 copy.wait()
-            if i == 0:
+            if i == min(1, per - 1):
                 load_w.wait()
             if i >= 1:
                 token_rows(i - 1, 1 - slot)

time: 303 us -> 303 us (level)
  no operation moved by 1% of the time
where the time goes in v5:
time: 303 us; the launch traced here: 299 us
  Pallas kernels  280 us (92%)
  other arithmetic  9.27 us (3%)
  local copies, waits for them, and re-layouts  8.41 us (3%)
    pallas_call x1, Pallas kernels, back(): pl.pallas_call(functools.partial(back_kernel, chips, depth, heads), out_s...  149 us
    pallas_call x1, Pallas kernels, forward(): pl.pallas_call(functools.partial(forward_kernel, chips, depth, heads), ou...  131 us

profile of v5, /device:TPU:0, one launch (start us, length us, event | category | flops | bytes accessed | tf_op | source)
XLA Modules:
  0.0 299.5 jit_solution(9155080471906926521)
XLA Ops:
  0.6 0.9 fusion.10
  1.6 0.8 convert_add_fusion
  2.3 0.6 reshape.132.vec_ref
  3.0 1.0 add_select_fusion
  4.0 0.6 fusion.1
  4.6 0.7 convert_element_type.78.pos_ref
  5.3 130.9 %forward.1 = (bf16[2,4,3,128,768]{4,3,2,1,0:T(8,128)(2,1)}, bf16[4,3,128,768]{3,2,1,0:T(8,128)(2,1)}, bf16[9,8,128,128]{3,2,1,0:T(8,128)(2,1)}, bf16[9,8,128,128...) custom-call(bf16[12,128,768]{2,1,0:T(8,128)(2,1)} %tok_ref.1, ...), custom_call_target="tpu_custom_call" | custom-call | tf_op jit(solution)/shard_map/forward/pallas_call | solution.py:1141
  136.2 149.4 %back.1 = (bf16[12,128,768]{2,1,0:T(8,128)(2,1)}, bf16[12,128,768]{2,1,0:T(8,128)(2,1)}, bf16[4,48,2304]{2,1,0:T(8,128)(2,1)}, bf16[2,4,24,768]{3,2,1,0:T(8,128)...) custom-call(bf16[9,8,128,128]{3,2,1,0:T(8,128)(2,1)} %get-tuple-elem, ...), custom_call_target="tpu_custom_call" | custom-call | tf_op jit(solution)/shard_map/back/pallas_call | solution.py:1980
  285.6 0.0 copy-start.2
  285.6 0.9 slice_reduce_fusion.1
  286.6 0.7 slice.56
  287.3 0.7 fusion.8
  288.0 2.8 bitcast_convert_fusion
  290.8 0.0 copy-start.3
  290.8 0.0 copy-done.2
  290.8 0.0 copy-start.4
  290.8 1.7 convert_element_type.83
  292.5 0.0 copy-start.5
  292.5 0.0 copy-start.1
  292.5 0.0 copy-done.3
  292.5 1.4 bitcast_convert_fusion.1
  293.9 0.0 copy-done.4
  293.9 0.9 bitcast_convert_fusion.2
  294.8 0.0 copy-done.5
  294.8 0.6 dynamic-slice_reduce_fusion
  295.4 0.0 copy-done.1
  295.4 0.0 copy-start
  295.4 1.4 copy.35
  296.8 1.1 copy-done
  297.9 1.4 copy.36
  (5 shorter events, 0.0 us)
Async XLA Ops:
  285.6 5.2 %copy-start.2 = (bf16[192,3072]{1,0:T(8,128)(2,1)S(1)}, bf16[192,3072]{1,0:T(8,128)(2,1)}, u32[]{:S(2)}) copy-start(bf16[192,3072]{1,0:T(8,128)(2,1)} %get-tuple-element.69) | copy-start | bytes 3538948
  290.8 1.7 copy-start.3
  290.8 3.1 %copy-start.4 = (bf16[2,4,24,768]{3,2,1,0:T(8,128)(2,1)S(1)}, bf16[2,4,24,768]{3,2,1,0:T(8,128)(2,1)}, u32[]{:S(2)}) copy-start(bf16[2,4,24,768]{3,2,1,0:T(8,128)(2,1)} %get-tuple-element.67) | copy-start | bytes 884740
  292.5 2.3 copy-start.5
  292.5 2.9 copy-start.1
  295.4 2.5 copy-start

commit v6 on v4

--- a/solution.py
+++ b/solution.py
@@ -1792,15 +1792,19 @@
         def step_sides():
             red.send_side()
 
+        def step_out_side():
+            out.send_side()
+
         hooks = {}
         steps = [
             (0, step_out_near),
             (1, step_exp_mid),
-            (3, step_red_mid),
-            (5, step_exp_last),
-            (6, step_red_last),
-            (7, step_out_last),
-            (8, step_sides),
+            (2, step_red_mid),
+            (4, step_exp_last),
+            (5, step_red_last),
+            (6, step_out_last),
+            (7, step_sides),
+            (8, step_out_side),
         ]
         for n, step in steps:
             hooks.setdefault(min(n, per * pairs - 1), []).append(step)
@@ -1839,7 +1843,7 @@
             slot = i % 2
             for copy in loads(i, slot):
                 copy.wait()
-            if i == 0:
+            if i == min(1, per - 1):
                 load_w.wait()
             if i >= 1:
                 token_rows(i - 1, 1 - slot)
@@ -1879,7 +1883,6 @@
         biases.send(1)
         token_rows(per - 1, (per - 1) % 2)
         emit(vbuf, vec_out)
-        out.send_side()
         for n in range(pairs - 1):
             atts[n].fold_mid()
             atts[n].send_last()

time: 303 us -> 309 us (1.020)
  Pallas kernels: 280 us -> 284 us
    pallas_call x1, Pallas kernels: 151 us -> 155 us  [back(): pl.pallas_call(functools.partial(back_kernel, chips, depth, heads), out_s...]
where the time goes in v6:
time: 309 us; the launch traced here: 304 us
  Pallas kernels  284 us (92%)
  other arithmetic  9.27 us (3%)
  local copies, waits for them, and re-layouts  8.41 us (3%)
    pallas_call x1, Pallas kernels, back(): pl.pallas_call(functools.partial(back_kernel, chips, depth, heads), out_s...  155 us
    pallas_call x1, Pallas kernels, forward(): pl.pallas_call(functools.partial(forward_kernel, chips, depth, heads), ou...  129 us

profile of v6, /device:TPU:0, one launch (start us, length us, event | category | flops | bytes accessed | tf_op | source)
XLA Modules:
  0.0 303.7 jit_solution(14878537021774297452)
XLA Ops:
  0.6 0.9 fusion.10
  1.6 0.8 convert_add_fusion
  2.3 0.6 reshape.132.vec_ref
  3.0 1.0 add_select_fusion
  4.0 0.6 fusion.1
  4.6 0.7 convert_element_type.78.pos_ref
  5.3 129.3 %forward.1 = (bf16[2,4,3,128,768]{4,3,2,1,0:T(8,128)(2,1)}, bf16[4,3,128,768]{3,2,1,0:T(8,128)(2,1)}, bf16[9,8,128,128]{3,2,1,0:T(8,128)(2,1)}, bf16[9,8,128,128...) custom-call(bf16[12,128,768]{2,1,0:T(8,128)(2,1)} %tok_ref.1, ...), custom_call_target="tpu_custom_call" | custom-call | tf_op jit(solution)/shard_map/forward/pallas_call | solution.py:1144
  134.6 155.1 %back.1 = (bf16[12,128,768]{2,1,0:T(8,128)(2,1)}, bf16[12,128,768]{2,1,0:T(8,128)(2,1)}, bf16[4,48,2304]{2,1,0:T(8,128)(2,1)}, bf16[2,4,24,768]{3,2,1,0:T(8,128)...) custom-call(bf16[9,8,128,128]{3,2,1,0:T(8,128)(2,1)} %get-tuple-elem, ...), custom_call_target="tpu_custom_call" | custom-call | tf_op jit(solution)/shard_map/back/pallas_call | solution.py:1986
  289.7 0.0 copy-start.2
  289.8 0.9 slice_reduce_fusion.1
  290.7 0.7 slice.56
  291.4 0.7 fusion.8
  292.1 2.8 bitcast_convert_fusion
  295.0 0.0 copy-start.3
  295.0 0.0 copy-done.2
  295.0 0.0 copy-start.4
  295.0 1.7 convert_element_type.83
  296.6 0.0 copy-start.5
  296.6 0.0 copy-start.1
  296.6 0.0 copy-done.3
  296.6 1.4 bitcast_convert_fusion.1
  298.0 0.0 copy-done.4
  298.0 0.9 bitcast_convert_fusion.2
  298.9 0.0 copy-done.5
  298.9 0.6 dynamic-slice_reduce_fusion
  299.5 0.0 copy-done.1
  299.5 0.0 copy-start
  299.5 1.4 copy.35
  300.9 1.1 copy-done
  302.0 1.4 copy.36
  (5 shorter events, 0.0 us)
Async XLA Ops:
  289.7 5.2 %copy-start.2 = (bf16[192,3072]{1,0:T(8,128)(2,1)S(1)}, bf16[192,3072]{1,0:T(8,128)(2,1)}, u32[]{:S(2)}) copy-start(bf16[192,3072]{1,0:T(8,128)(2,1)} %get-tuple-element.69) | copy-start | bytes 3538948
  295.0 1.7 copy-start.3
  295.0 3.1 %copy-start.4 = (bf16[2,4,24,768]{3,2,1,0:T(8,128)(2,1)S(1)}, bf16[2,4,24,768]{3,2,1,0:T(8,128)(2,1)}, u32[]{:S(2)}) copy-start(bf16[2,4,24,768]{3,2,1,0:T(8,128)(2,1)} %get-tuple-element.67) | copy-start | bytes 884740
  296.6 2.3 copy-start.5
  296.6 2.9 copy-start.1
  299.5 2.5 copy-start
